TPU v7x, 32 devices: a whole 2x2x4 slice. The times are simulated.
32 devices in a mesh: groups: 2 (over y), section: 4 (over z), replica: 2 (over x), tensor: 2 (over core).
Axes of the slice: x: 2, y: 2, z: 4, core: 2. Of those that a mesh axis runs over, the one named last changes fastest.
Arguments:
- inflow: bfloat16 [4, 1024, 1152], P('section', ('groups', 'replica')), parts along dimension 1, may hold values from -6 to 6
- fresh_rows: bfloat16 [2, 4, 256, 1152], P(None, ('groups', 'replica'), 'section'), parts along dimension 1, may hold values from -6 to 6
- lin_weight: bfloat16 [4, 1152, 1152], P('section', None, 'tensor'), may hold values from -0.125 to 0.125
- qkv_weight: bfloat16 [4, 3, 1152, 576], P('section', None, None, 'tensor'), may hold values from -2 to 2
- out_weight: bfloat16 [4, 576, 1152], P('section', 'tensor'), may hold values from -0.25 to 0.25
- mod_weight: bfloat16 [4, 128, 2, 1152], P('section', None, None, 'tensor'), may hold values from -0.5 to 0.5
- plan: int32 [3, 4], P(None, 'section'), may hold values from 0 to 5
- timesteps: int32 [6, 4], P(None, ('groups', 'replica')), parts along dimension 1, may hold values from 0 to 999
Outputs:
- settled: float32 [4, 1024, 1152], P('section', ('groups', 'replica'), 'tensor'), parts along dimension 1
There are 2 independent parts, one for each index of `groups`. A program takes and returns all parts, laid end to end along the dimension named above; an argument that names none is the same for every part. Nothing has to cross between parts.
All inputs are finite; a program needn't handle non-finite values.
Results may differ from a plain program's by a relative error of at most 0.039.
Values may be sent and summed in bfloat16 or wider, within the bound.
No kernel may reach another device: no remote copies, remote signals or barrier semaphores. Data moves between devices by JAX's collectives and lax.ppermute only.
A program may use at most 64 MiB of HBM per device.

v0:
```python
import functools
import math

import jax
import jax.numpy as jnp
from jax import lax
from jax.experimental import pallas as pl
from jax.experimental.pallas import tpu as pltpu
from jax.sharding import PartitionSpec as P


DH = 72
FREQ = 128
TICKS = 3
EPSILON = 1e-06


VMEM = pl.BlockSpec(memory_space=pltpu.VMEM)
SMEM = pl.BlockSpec(memory_space=pltpu.SMEM)
ANY = pl.BlockSpec(memory_space=pl.ANY)
HBM = pl.BlockSpec(memory_space=pltpu.HBM)
TICK_LANES = 32
CHUNK = 96
PLACES = 3
FULL = 24 << 20


def call(body, outs, in_specs, flops, args, scratch=(), limit=24 << 20):
    moved = sum(math.prod(a.shape) * a.dtype.itemsize for a in (*args, *outs))
    return pl.pallas_call(
        body,
        out_shape=tuple(outs),
        in_specs=in_specs,
        out_specs=tuple(VMEM for _ in outs),
        scratch_shapes=list(scratch),
        compiler_params=pltpu.CompilerParams(vmem_limit_bytes=limit),
        cost_estimate=pl.CostEstimate(flops=flops, bytes_accessed=moved, transcendentals=0),
    )(*args)


def like(shape, dtype):
    return jax.ShapeDtypeStruct(shape, dtype)


def halves(tensor_index, half):
    own = pl.ds(pl.multiple_of(tensor_index * half, 16), half)
    other = pl.ds(pl.multiple_of((1 - tensor_index) * half, 16), half)
    return own, other


def column(ref, tick, rows=slice(None)):
    lane = tick * TICK_LANES
    return ref[rows, lane : lane + 1].astype(jnp.float32)


def folded(value):
    return jnp.sum(value.reshape(-1, 8, value.shape[-1]), axis=0)


def normalise(load, store, scale_ref, tick):
    count = scale_ref.shape[0]
    chunks = [slice(start, start + CHUNK) for start in range(0, count, CHUNK)]
    total = None
    for rows in chunks:
        part = folded(load(rows))
        total = part if total is None else total + part
    mean = jnp.sum(total, axis=0, keepdims=True) * (1.0 / count)
    total = None
    for rows in chunks:
        centred = load(rows) - mean
        part = folded(centred * centred)
        total = part if total is None else total + part
    variance = jnp.sum(total, axis=0, keepdims=True) * (1.0 / count)
    inverse = lax.rsqrt(variance + EPSILON)
    for rows in chunks:
        normed = (load(rows) - mean) * inverse
        store(rows, (normed * (1.0 + column(scale_ref, tick, rows))).astype(jnp.bfloat16))


def storing(ref):
    def store(rows, value):
        ref[rows, :] = value

    return store


def first_kernel(
    where, mod_own_hbm, mod_other_hbm, x_hbm,
    scale_ref, gate_ref, own_ref, other_ref, hidden_ref,
    mod_own, mod_other, x_ref, turned, sems,
):
    copies = [
        pltpu.make_async_copy(source, target, sems.at[index])
        for index, (source, target) in enumerate(
            ((mod_own_hbm, mod_own), (mod_other_hbm, mod_other), (x_hbm, x_ref))
        )
    ]
    for copy in copies:
        copy.start()
    half_freq = FREQ // 2
    lanes = scale_ref.shape[1]
    position = lax.broadcasted_iota(jnp.int32, (half_freq, lanes), 0).astype(jnp.float32)
    lane = lax.broadcasted_iota(jnp.int32, (half_freq, lanes), 1)
    frequency = jnp.exp(-math.log(10000.0) * position / half_freq)
    stamp = jnp.zeros((half_freq, lanes), jnp.float32)
    for tick in range(TICKS):
        moment = where[PLACES + TICKS + where[PLACES + tick]].astype(jnp.float32)
        stamp = jnp.where(lane // TICK_LANES == tick, moment, stamp)
    phases = stamp * frequency
    rest = jnp.concatenate([jnp.cos(phases), jnp.sin(phases)], axis=0)
    parts = []
    for _ in range(3):
        part = rest.astype(jnp.bfloat16)
        parts.append(part)
        rest = rest - part.astype(jnp.float32)
    stacked = jnp.concatenate(parts, axis=0)
    for copy in copies:
        copy.wait()
    half = mod_own.shape[1]
    for ref, rows in zip((mod_own, mod_other), halves(where[0], half)):
        for kind, target in enumerate((scale_ref, gate_ref)):
            weight = jnp.concatenate([ref[kind]] * 3, axis=1)
            product = jnp.dot(weight, stacked, preferred_element_type=jnp.float32)
            target[rows, :] = product.astype(jnp.bfloat16)
    tokens = own_ref.shape[1]
    turned[...] = jnp.transpose(x_ref[...].astype(jnp.float32), (1, 0))
    for index in range(2):
        columns = slice(index * tokens, (index + 1) * tokens)

        @pl.when(where[0] == index)
        def _():
            normalise(lambda rows: turned[rows, columns], storing(own_ref), scale_ref, 0)
            hidden_ref[...] = turned[:, columns].astype(jnp.bfloat16)

        @pl.when(where[0] != index)
        def _():
            normalise(lambda rows: turned[rows, columns], storing(other_ref), scale_ref, 0)


def norm_kernel(tick, where, arrived_ref, scale_ref, order_ref, *refs):
    *blocks, current_ref, mixed_ref, later_ref = refs

    @pl.when(where[2] == 0)
    def _():
        for index, target in enumerate((current_ref, later_ref)):
            head = jnp.where(
                where[0] == 0, blocks[0][index].astype(jnp.float32), blocks[1][index].astype(jnp.float32)
            )
            rows = [head] + [ref[index].astype(jnp.float32) for ref in blocks[2:]]
            target[...] = jnp.transpose(jnp.concatenate(rows, axis=0), (1, 0)).astype(jnp.bfloat16)

    @pl.when(where[2] != 0)
    def _():
        current_ref[...] = arrived_ref[...]

    normalise(lambda rows: current_ref[rows, :].astype(jnp.float32), storing(mixed_ref), scale_ref, tick)


def product_kernel(where, x_ref, own_ref, other_ref, *results):
    half = own_ref.shape[0]
    for ref, rows in zip((own_ref, other_ref), halves(where[0], half)):
        product = jnp.dot(ref[...], x_ref[...], preferred_element_type=jnp.float32)
        for result in results:
            result[rows, :] = product.astype(result.dtype)


def lowest_kernel(where, x_ref, own_ref, other_ref, order_ref, narrow_ref):
    @pl.when(where[2] == 0)
    def _():
        product_kernel(where, x_ref, own_ref, other_ref, narrow_ref)


def skip_kernel(where, x_ref, own_ref, other_ref, order_ref, narrow_ref):
    product_kernel(where, x_ref, own_ref, other_ref, narrow_ref)


def chosen_kernel(middle, where, low_ref, high_ref, own_ref, other_ref, wide_ref):
    half = own_ref.shape[0]
    value = jnp.where(where[2] == middle, low_ref[...], high_ref[...])
    for ref, rows in zip((own_ref, other_ref), halves(where[0], half)):
        wide_ref[rows, :] = jnp.dot(ref[...], value, preferred_element_type=jnp.float32)


def joined_kernel(tick, where, product_ref, skip_ref, scale_ref, order_ref, mixed_ref, hidden_ref):
    for start in range(0, product_ref.shape[0], CHUNK):
        rows = slice(start, start + CHUNK)
        hidden_ref[rows, :] = product_ref[rows, :] + skip_ref[rows, :].astype(jnp.float32)
    normalise(lambda rows: hidden_ref[rows, :], storing(mixed_ref), scale_ref, tick)


def last_joined_kernel(
    tick, last, where, fresh_ref, low_ref, product_ref, skip_ref, low_skip_ref, scale_ref, mixed_ref, hidden_ref
):
    @pl.when((where[1] == 1) & (where[2] == last))
    def _():
        hidden_ref[...] = product_ref[...] + low_skip_ref[...].astype(jnp.float32)

    @pl.when((where[1] == 1) & (where[2] != last))
    def _():
        hidden_ref[...] = product_ref[...] + skip_ref[...].astype(jnp.float32)

    @pl.when((where[1] == 0) & (where[2] == 0))
    def _():
        hidden_ref[...] = fresh_ref[...].astype(jnp.float32)

    @pl.when((where[1] == 0) & (where[2] != 0))
    def _():
        hidden_ref[...] = low_ref[...].astype(jnp.float32)

    normalise(lambda rows: hidden_ref[rows, :], storing(mixed_ref), scale_ref, tick)


def block_kernel(
    tick, stage, where, own_ref, other_ref, hidden_ref, gate_ref, qkv_own, qkv_other, out_own, out_other, *rest
):
    if stage == "first":
        *results, scores, raised, attended, held_a, held_b, raw_a, raw_b, sems = rest
        copies = [
            pltpu.make_async_copy(source, target, sems.at[index])
            for index, (source, target) in enumerate(
                ((qkv_own, held_a), (qkv_other, held_b), (out_own, raw_a), (out_other, raw_b))
            )
        ]
        for copy in copies:
            copy.start()
        projections, turned = (held_a, held_b), results[1:]
    else:
        *results, scores, raised, attended = rest
        projections, turned = (qkv_own, qkv_other), (out_own, out_other)
    own = own_ref[...]
    both = jnp.concatenate([own, other_ref[...]], axis=1)
    head_cols = projections[0].shape[1]
    heads = head_cols // DH
    values = []
    for group, ref in enumerate(projections):
        if stage == "first":
            copies[group].wait()
        query = jnp.dot(ref[0], own, preferred_element_type=jnp.float32).astype(jnp.bfloat16)
        key = jnp.dot(ref[1], both, preferred_element_type=jnp.float32).astype(jnp.bfloat16)
        values.append(jnp.dot(ref[2], both, preferred_element_type=jnp.float32).astype(jnp.bfloat16))
        for head in range(heads):
            rows = slice(head * DH, (head + 1) * DH)
            scores[group * heads + head] = lax.dot_general(
                key[rows], query[rows], (((0,), (0,)), ((), ())), preferred_element_type=jnp.float32
            ) * (1.0 / math.sqrt(DH))
    if stage == "first":
        for index, (source, target) in enumerate(zip((raw_a, raw_b), turned)):
            copies[2 + index].wait()
            target[...] = jnp.transpose(source[...].astype(jnp.float32), (1, 0)).astype(jnp.bfloat16)
    weights = []
    for head in range(2 * heads):
        value = scores[head]
        power = jnp.exp(value - jnp.max(value, axis=0, keepdims=True))
        weights.append(jnp.sum(power, axis=0, keepdims=True))
        raised[head] = power.astype(jnp.bfloat16)
    total = None
    for group, out_ref in enumerate(turned):
        for head in range(heads):
            rows = slice(head * DH, (head + 1) * DH)
            place = group * heads + head
            attended[place * DH : (place + 1) * DH, :] = (
                jnp.dot(values[group][rows], raised[place], preferred_element_type=jnp.float32) / weights[place]
            )
        rows = slice(group * head_cols, (group + 1) * head_cols)
        term = jnp.dot(out_ref[...], attended[rows, :].astype(jnp.bfloat16), preferred_element_type=jnp.float32)
        term = term.astype(jnp.bfloat16).astype(jnp.float32)
        total = term if total is None else total + term
    result = hidden_ref[...].astype(jnp.float32) + column(gate_ref, tick) * total
    if stage == "last":
        kept_ref, sent_ref, full_ref = results
        full_ref[...] = result
        own_rows, other_rows = halves(where[0], kept_ref.shape[0])
        kept_ref[...] = full_ref[own_rows, :]
        sent_ref[...] = full_ref[other_rows, :]
    else:
        results[0][...] = result.astype(jnp.bfloat16)


def relayed(inflow, fresh_rows, lin_weight, qkv_weight, out_weight, mod_weight, plan, timesteps):
    sections = lax.axis_size("section")
    middle = sections // 2
    section = lax.axis_index("section")
    core = lax.axis_index("tensor")
    _, row_count, width = inflow.shape
    tokens = row_count // lax.axis_size("tensor")
    half = lin_weight.shape[2]
    head_cols = out_weight.shape[1]
    if lax.axis_size("tensor") != 2 or timesteps.shape[1] != 1 or sections < 4:
        raise ValueError("unsupported split")
    where = jnp.concatenate(
        [jnp.stack([core, (section >= middle).astype(jnp.int32), section]), plan[:, 0], timesteps[:, 0]]
    ).astype(jnp.int32)

    def swapped(value):
        return lax.ppermute(value, "tensor", [(0, 1), (1, 0)])

    def moved(value, pairs):
        return lax.ppermute(value, "section", pairs)

    mod_own = jnp.transpose(mod_weight[0], (1, 2, 0))
    qkv_own = jnp.transpose(qkv_weight[0], (0, 2, 1))
    lin_own = jnp.transpose(lin_weight[0], (1, 0))
    out_own = out_weight[0]
    mod_other = swapped(mod_own)
    qkv_other = swapped(qkv_own)
    out_other = swapped(out_own)

    narrow = like((width, tokens), jnp.bfloat16)
    wide = like((width, tokens), jnp.float32)
    lanes = like((width, 128), jnp.bfloat16)
    turned = like((width, head_cols), jnp.bfloat16)
    product_flops = 2 * width * width * tokens
    norm_flops = 12 * width * tokens
    block_flops = 6 * product_flops

    scale, gate, own, other, hidden = call(
        first_kernel, [lanes, lanes, narrow, narrow, narrow], [SMEM] + [HBM] * 3, 4 * norm_flops,
        (where, mod_own, mod_other, inflow[0]),
        [
            pltpu.VMEM(mod_own.shape, jnp.bfloat16),
            pltpu.VMEM(mod_own.shape, jnp.bfloat16),
            pltpu.VMEM((row_count, width), jnp.bfloat16),
            pltpu.VMEM((width, row_count), jnp.float32),
            pltpu.SemaphoreType.DMA((3,)),
        ],
        FULL,
    )

    def attention(own, other, hidden, outs, tick, stage):
        results = [narrow]
        count = 2 * head_cols // DH
        scratch = [
            pltpu.VMEM((count, row_count, tokens), jnp.float32),
            pltpu.VMEM((count, row_count, tokens), jnp.bfloat16),
            pltpu.VMEM((2 * head_cols, tokens), jnp.float32),
        ]
        weights = [VMEM] * 4
        if stage == "first":
            results = [narrow, turned, turned]
            weights = [HBM] * 4
            scratch += [pltpu.VMEM(qkv_own.shape, jnp.bfloat16)] * 2
            scratch += [pltpu.VMEM(out_own.shape, jnp.bfloat16)] * 2
            scratch += [pltpu.SemaphoreType.DMA((4,))]
        if stage == "last":
            results = [like((half, tokens), jnp.float32)] * 2
            scratch = [pltpu.VMEM((width, tokens), jnp.float32)] + scratch
        return call(
            functools.partial(block_kernel, tick, stage), results, [SMEM] + [VMEM] * 4 + weights, block_flops,
            (where, own, other, hidden, gate, qkv_own, qkv_other, *outs), scratch,
            FULL if stage == "first" else 24 << 20,
        )

    early = middle <= sections - TICKS
    if early:
        lin_other = swapped(lin_own)
        products, outgoing = call(
            product_kernel, [wide, narrow], [SMEM] + [VMEM] * 3, product_flops,
            (where, hidden, lin_own, lin_other),
        )
        skip = moved(outgoing, [(low, sections - 1 - low) for low in range(middle)])
        mixed, joined = call(
            functools.partial(joined_kernel, 0), [narrow, wide], [SMEM] + [VMEM] * 3 + [ANY], norm_flops,
            (where, products, skip, scale, skip),
        )
        upper = section >= middle
        own = jnp.where(upper, mixed, own)
        hidden = jnp.where(upper, joined, hidden.astype(jnp.float32))
        other = swapped(own)
    settled, *outs = attention(own, other, hidden, (out_own, out_other), 0, "first")

    arrived = moved(settled, [(low, low + 1) for low in range(sections - 2)])
    fresh_block, lin_source, _ = lax.optimization_barrier((fresh_rows[:, 0], lin_own, settled))
    if not early:
        lin_other = swapped(lin_source)
    blocks = [fresh_block]
    for place in range(middle):
        pairs = [
            ((side * middle + place) * 2 + side, side) for side in range(2) if side or place
        ]
        blocks.append(lax.ppermute(fresh_block, ("section", "tensor"), pairs))
    products, outgoing = call(
        product_kernel, [wide, narrow], [SMEM] + [VMEM] * 3, product_flops,
        (where, arrived, lin_own, lin_other),
    )
    skip = moved(outgoing, [(low, sections - 1 - low) for low in range(1, middle)])
    current, own, later = call(
        functools.partial(norm_kernel, 1), [narrow] * 3, [SMEM] + [VMEM] * 2 + [ANY] + [VMEM] * len(blocks), norm_flops,
        (where, arrived, scale, outgoing, *blocks),
    )
    other = swapped(own)
    down = attention(own, other, current, outs, 1, "middle")[0]
    arrived_low = moved(down, [(low, low + 1) for low in range(middle)])
    lowest = call(
        lowest_kernel, [narrow], [SMEM] + [VMEM] * 3 + [ANY], product_flops,
        (where, later, lin_own, lin_other, down),
    )[0]
    low_skip = moved(lowest, [(0, sections - 1)])
    own, hidden = call(
        functools.partial(joined_kernel, 1), [narrow, wide], [SMEM] + [VMEM] * 3 + [ANY], norm_flops,
        (where, products, skip, scale, lowest),
    )
    other = swapped(own)
    up = attention(own, other, hidden, outs, 1, "middle")[0]

    arrived_high = moved(up, [(low, low + 1) for low in range(middle, sections - 1)])
    outgoing = call(
        skip_kernel, [narrow], [SMEM] + [VMEM] * 3 + [ANY], product_flops,
        (where, arrived_low, lin_own, lin_other, up),
    )[0]
    skip = moved(outgoing, [(low, sections - 1 - low) for low in range(1, middle)])
    products = call(
        functools.partial(chosen_kernel, middle), [wide], [SMEM] + [VMEM] * 4, product_flops,
        (where, arrived_low, arrived_high, lin_own, lin_other),
    )[0]
    own, hidden = call(
        functools.partial(last_joined_kernel, 2, sections - 1), [narrow, wide], [SMEM] + [VMEM] * 6, norm_flops,
        (where, later, arrived_low, products, skip, low_skip, scale),
    )
    other = swapped(own)
    kept, sent = attention(own, other, hidden, outs, 2, "last")
    received = swapped(sent)
    columns = jnp.where(
        core == 0,
        jnp.concatenate([kept, received], axis=1),
        jnp.concatenate([received, kept], axis=1),
    )
    return jnp.transpose(columns, (1, 0))[None]


def solution(mesh):
    return jax.shard_map(
        relayed,
        mesh=mesh,
        in_specs=(
            P("section", ("groups", "replica"), None),
            P(None, ("groups", "replica"), "section", None),
            P("section", None, "tensor"),
            P("section", None, None, "tensor"),
            P("section", "tensor", None),
            P("section", None, None, "tensor"),
            P(None, "section"),
            P(None, ("groups", "replica")),
        ),
        out_specs=P("section", ("groups", "replica"), "tensor"),
        check_vma=False,
    )
```

profile of v0, /device:TPU:17, one launch (start us, length us, event | category | flops | bytes accessed | tf_op | source)
XLA Modules:
  0.0 83.2 jit_solution(11454648454639804313)
XLA Ops:
  0.0 0.7 collective-permute-start.1
  0.7 0.0 collective-permute-start.2
  0.7 0.5 collective-permute-start
  1.2 0.7 concatenate.9.where
  1.9 4.0 %collective-permute-done.mod_other_hbm = bf16[2,576,128]{2,1,0:T(8,128)(2,1)S(1)} collective-permute-done((bf16[2,576,128]{2,1,0:T(8,128)(2,1)}, bf16[2,576,128]{2,1,0:T(8,128)(2,1)S(1)}, u32[]{:S(2)}, u32[]{:S(2)}) %collective-permute-start) | collective-permute-done | bytes 294944 | tf_op jit(solution)/shard_map/ppermute | solution.py:295
  5.9 0.0 copy-start.1
  5.9 1.1 %copy-done.1 = bf16[1,256,1152]{2,1,0:T(8,128)(2,1)S(1)} copy-done((bf16[1,256,1152]{2,1,0:T(8,128)(2,1)S(1)}, bf16[1,256,1152]{2,1,0:T(8,128)(2,1)}, u32[]{:S(2)}) %copy-start.1) | copy-done | bytes 589848
  7.0 0.0 copy-start.2
  7.0 1.0 %copy-done.2 = bf16[1,128,2,576]{1,3,2,0:T(8,128)(2,1)S(1)} copy-done((bf16[1,128,2,576]{1,3,2,0:T(8,128)(2,1)S(1)}, bf16[1,128,2,576]{1,3,2,0:T(8,128)(2,1)}, u32[]{:S(2)}) %copy-start.2) | copy-done | bytes 294936
  7.9 2.1 %shard_map.82 = (bf16[1152,128]{1,0:T(8,128)(2,1)S(1)}, bf16[1152,128]{1,0:T(8,128)(2,1)S(1)}, bf16[1152,128]{1,0:T(8,128)(2,1)S(1)}, bf16[1152,128]{1,0:T(8,128)(2,1)S(1)}, bf16[1152,128]{1,0:T(8,128)(2,1)S(1)}) custom-call(s32[12]{0:T(128)S(1)} %concatenate.9.where, bf16[2,576,128]{2,1,0:T(8,128)(2,1)S(1)} %bitcast.28, ...), custom_call_target="tpu_custom_call" | custom-call | flops 7077888 | bytes 2654256 | tf_op jit(solution)/shard_map/pallas_call | solution.py:30
  10.1 0.0 collective-permute-done.2.out_other
  10.1 0.0 collective-permute-done.1.qkv_other
  10.1 0.0 copy-start.4
  10.1 1.5 %copy-done.4 = bf16[1,3,1152,288]{2,3,1,0:T(8,128)(2,1)S(1)} copy-done((bf16[1,3,1152,288]{2,3,1,0:T(8,128)(2,1)S(1)}, bf16[1,3,1152,288]{2,3,1,0:T(8,128)(2,1)}, u32[]{:S(2)}) %copy-start.4) | copy-done | bytes 1990680
  11.6 0.0 copy-start.6
  11.6 1.1 %copy-done.6 = bf16[1,288,1152]{2,1,0:T(8,128)(2,1)S(1)} copy-done((bf16[1,288,1152]{2,1,0:T(8,128)(2,1)S(1)}, bf16[1,288,1152]{2,1,0:T(8,128)(2,1)}, u32[]{:S(2)}) %copy-start.6) | copy-done | bytes 663576
  12.7 0.0 copy-start
  12.7 0.0 copy-start.3
  12.7 4.9 %shard_map.83 = (bf16[1152,128]{1,0:T(8,128)(2,1)S(1)}, bf16[1152,288]{1,0:T(8,128)(2,1)S(1)}, bf16[1152,288]{1,0:T(8,128)(2,1)S(1)}) custom-call(s32[12]{0:T(128)S(1)} %concatenate.9.where, bf16[1152,128]{1,0:T(8,128)(2,1)S(1)} %get-tuple-element.26.own_ref, bf16[1152,128]{1,0:T(8,128)(2,1)S(1)} %get-tuple-element.27.other_ref, ...), custom_call_target="tpu_custom_call" | custom-call | flops 2038431744 | bytes 8110128 | tf_op jit(solution)/shard_map/pallas_call | solution.py:30
  17.7 0.0 copy-done
  17.7 0.0 copy-start.5
  17.7 0.5 collective-permute-start.4
  18.2 1.4 %collective-permute-start.3 = (bf16[1152,128]{1,0:T(8,128)(2,1)S(1)}, bf16[1152,128]{1,0:T(8,128)(2,1)S(1)}, u32[]{:S(2)}, u32[]{:S(2)}) collective-permute-start(bf16[1152,128]{1,0:T(8,128)(2,1)S(1)} %get-tuple-element.30), channel_id=1, source_target_pairs={{0,4},{4,8},{1,5},{5,9},{2,6},{6,10},{3,7},{7,11},{16,20},{20,24},... | collective-permute-start | bytes 884744 | tf_op jit(solution)/shard_map/ppermute | solution.py:298
  19.6 0.0 copy-done.3
  19.6 3.9 %collective-permute-start.5 = (bf16[2,64,1152]{2,1,0:T(8,128)(2,1)S(1)}, bf16[2,64,1152]{2,1,0:T(8,128)(2,1)S(1)}, u32[]{:S(2)}, u32[]{:S(2)}) collective-permute-start(bf16[2,64,1152]{2,1,0:T(8,128)(2,1)S(1)} %bitcast.29), channel_id=1, source_target_pairs={{9,1},{11,3},{25,17},{27,19}} | collective-permute-start | bytes 884744 | tf_op jit(solution)/shard_map/ppermute | solution.py:380
  23.5 0.7 collective-permute-start.6
  24.2 4.4 %collective-permute-done.3.x_ref.arrived_ref = bf16[1152,128]{1,0:T(8,128)(2,1)S(1)} collective-permute-done((bf16[1152,128]{1,0:T(8,128)(2,1)S(1)}, bf16[1152,128]{1,0:T(8,128)(2,1)S(1)}, u32[]{:S(2)}, u32[]{:S(2)}) %collective-permute-start.3) | collective-permute-done | bytes 294944 | tf_op jit(solution)/shard_map/ppermute | solution.py:298
  28.6 0.0 collective-permute-done.4.other_ref
  28.6 1.4 %shard_map.84 = (f32[1152,128]{1,0:T(8,128)S(1)}, bf16[1152,128]{1,0:T(8,128)(2,1)S(1)}) custom-call(s32[12]{0:T(128)S(1)} %concatenate.9.where, bf16[1152,128]{1,0:T(8,128)(2,1)S(1)} %collective-permute-done.3.x_ref.arrived_ref, bf16[576,1152]{1,0:T(8,128)(2,1)S(1)} %bitcast.22, bf16[576,1152]{1,0:T(8,128)(2,1)S(1)} %collective-permute-done.4.other_ref), custom_call_target="tpu_custom_call" | custom-call | flops 339738624 | bytes 3833904 | tf_op jit(solution)/shard_map/pallas_call | solution.py:30
  30.0 0.3 collective-permute-done.5.refs_1_
  30.3 0.0 collective-permute-done.6.refs_2_
  30.3 0.9 %shard_map.85 = (bf16[1152,128]{1,0:T(8,128)(2,1)S(1)}, bf16[1152,128]{1,0:T(8,128)(2,1)S(1)}, bf16[1152,128]{1,0:T(8,128)(2,1)S(1)}) custom-call(s32[12]{0:T(128)S(1)} %concatenate.9.where, bf16[1152,128]{1,0:T(8,128)(2,1)S(1)} %collective-permute-done.3.x_ref.arrived_ref, bf16[1152,128]{1,0:T(8,128)(2,1)S(1)} %get-tuple-element.31.scale_ref, ...), custom_call_target="tpu_custom_call" | custom-call | flops 1769472 | bytes 2654256 | tf_op jit(solution)/shard_map/pallas_call | solution.py:30
  31.2 0.7 collective-permute-start.7
  32.0 1.3 %collective-permute-start.9 = (bf16[1152,128]{1,0:T(8,128)(2,1)S(1)}, bf16[1152,128]{1,0:T(8,128)(2,1)S(1)}, u32[]{:S(2)}, u32[]{:S(2)}) collective-permute-start(bf16[1152,128]{1,0:T(8,128)(2,1)S(1)} %get-tuple-element.33.order_ref), channel_id=1, source_target_pairs={{4,8},{5,9},{6,10},{7,11},{20,24},{21,25},{22,26},{23,27}} | collective-permute-start | bytes 884744 | tf_op jit(solution)/shard_map/ppermute | solution.py:298
  33.2 0.0 collective-permute-done.7.other_ref
  33.3 0.0 copy-done.5
  33.3 2.9 %shard_map.86.order_ref = bf16[1152,128]{1,0:T(8,128)(2,1)S(1)} custom-call(s32[12]{0:T(128)S(1)} %concatenate.9.where, bf16[1152,128]{1,0:T(8,128)(2,1)S(1)} %get-tuple-element.36.own_ref, bf16[1152,128]{1,0:T(8,128)(2,1)S(1)} %collective-permute-done.7.other_ref, bf16[1152,128]{1,0:T(8,128)(2,1)S(1)} %get-tuple-element.37.hidden_ref, ...), custom_call_target="tpu_custom_call" | custom-call | flops 2038431744 | bytes 6783024 | tf_op jit(solution)/shard_map/pallas_call | solution.py:30
  36.2 0.6 shard_map.87.order_ref
  36.7 7.9 %collective-permute-done.9.skip_ref = bf16[1152,128]{1,0:T(8,128)(2,1)S(1)} collective-permute-done((bf16[1152,128]{1,0:T(8,128)(2,1)S(1)}, bf16[1152,128]{1,0:T(8,128)(2,1)S(1)}, u32[]{:S(2)}, u32[]{:S(2)}) %collective-permute-start.9) | collective-permute-done | bytes 294944 | tf_op jit(solution)/shard_map/ppermute | solution.py:298
  44.6 0.9 %shard_map.88 = (bf16[1152,128]{1,0:T(8,128)(2,1)S(1)}, f32[1152,128]{1,0:T(8,128)S(1)}) custom-call(s32[12]{0:T(128)S(1)} %concatenate.9.where, f32[1152,128]{1,0:T(8,128)S(1)} %get-tuple-element.40.product_ref, bf16[1152,128]{1,0:T(8,128)(2,1)S(1)} %collective-permute-done.9.skip_ref, bf16[1152,128]{1,0:T(8,128)(2,1)S(1)} %get-tuple-element.31.scale_ref, ...), custom_call_target="tpu_custom_call" | custom-call | flops 1769472 | bytes 2359344 | tf_op jit(solution)/shard_map/pallas_call | solution.py:30
  45.5 0.7 collective-permute-start.10
  46.1 1.3 %collective-permute-start.8 = (bf16[1152,128]{1,0:T(8,128)(2,1)S(1)}, bf16[1152,128]{1,0:T(8,128)(2,1)S(1)}, u32[]{:S(2)}, u32[]{:S(2)}) collective-permute-start(bf16[1152,128]{1,0:T(8,128)(2,1)S(1)} %shard_map.86.order_ref), channel_id=1, source_target_pairs={{0,4},{4,8},{1,5},{5,9},{2,6},{6,10},{3,7},{7,11},{16,20},{20,24},... | collective-permute-start | bytes 884744 | tf_op jit(solution)/shard_map/ppermute | solution.py:298
  47.4 0.9 %collective-permute-start.13 = (bf16[1152,128]{1,0:T(8,128)(2,1)S(1)}, bf16[1152,128]{1,0:T(8,128)(2,1)S(1)}, u32[]{:S(2)}, u32[]{:S(2)}) collective-permute-start(bf16[1152,128]{1,0:T(8,128)(2,1)S(1)} %shard_map.87.order_ref), channel_id=1, source_target_pairs={{0,12},{1,13},{2,14},{3,15},{16,28},{17,29},{18,30},{19,31}} | collective-permute-start | bytes 884744 | tf_op jit(solution)/shard_map/ppermute | solution.py:298
  48.3 0.0 collective-permute-done.10.other_ref
  48.3 2.9 %shard_map.89.order_ref = bf16[1152,128]{1,0:T(8,128)(2,1)S(1)} custom-call(s32[12]{0:T(128)S(1)} %concatenate.9.where, bf16[1152,128]{1,0:T(8,128)(2,1)S(1)} %get-tuple-element.41.own_ref, bf16[1152,128]{1,0:T(8,128)(2,1)S(1)} %collective-permute-done.10.other_ref, f32[1152,128]{1,0:T(8,128)S(1)} %get-tuple-element.42.hidden_ref, ...), custom_call_target="tpu_custom_call" | custom-call | flops 2038431744 | bytes 7077936 | tf_op jit(solution)/shard_map/pallas_call | solution.py:30
  51.2 1.3 %collective-permute-start.11 = (bf16[1152,128]{1,0:T(8,128)(2,1)S(1)}, bf16[1152,128]{1,0:T(8,128)(2,1)S(1)}, u32[]{:S(2)}, u32[]{:S(2)}) collective-permute-start(bf16[1152,128]{1,0:T(8,128)(2,1)S(1)} %shard_map.89.order_ref), channel_id=1, source_target_pairs={{8,12},{9,13},{10,14},{11,15},{24,28},{25,29},{26,30},{27,31}} | collective-permute-start | bytes 884744 | tf_op jit(solution)/shard_map/ppermute | solution.py:298
  52.5 10.3 %collective-permute-done.8.low_ref.x_ref = bf16[1152,128]{1,0:T(8,128)(2,1)S(1)} collective-permute-done((bf16[1152,128]{1,0:T(8,128)(2,1)S(1)}, bf16[1152,128]{1,0:T(8,128)(2,1)S(1)}, u32[]{:S(2)}, u32[]{:S(2)}) %collective-permute-start.8) | collective-permute-done | bytes 294944 | tf_op jit(solution)/shard_map/ppermute | solution.py:298
  62.9 1.4 %shard_map.91 = bf16[1152,128]{1,0:T(8,128)(2,1)S(1)} custom-call(s32[12]{0:T(128)S(1)} %concatenate.9.where, bf16[1152,128]{1,0:T(8,128)(2,1)S(1)} %collective-permute-done.8.low_ref.x_ref, bf16[576,1152]{1,0:T(8,128)(2,1)S(1)} %bitcast.24, bf16[576,1152]{1,0:T(8,128)(2,1)S(1)} %collective-permute-done.4.other_ref, bf16[1152,128]{1,0:T(8,128)(2,1)S(1)} %shard_map.89.order_ref), custom_call_target="tpu_custom_call" | custom-call | flops 339738624 | bytes 3538992 | tf_op jit(solution)/shard_map/pallas_call | solution.py:30
  64.3 1.3 %collective-permute-start.12 = (bf16[1152,128]{1,0:T(8,128)(2,1)S(1)}, bf16[1152,128]{1,0:T(8,128)(2,1)S(1)}, u32[]{:S(2)}, u32[]{:S(2)}) collective-permute-start(bf16[1152,128]{1,0:T(8,128)(2,1)S(1)} %shard_map.91), channel_id=1, source_target_pairs={{4,8},{5,9},{6,10},{7,11},{20,24},{21,25},{22,26},{23,27}} | collective-permute-start | bytes 884744 | tf_op jit(solution)/shard_map/ppermute | solution.py:298
  65.6 0.0 collective-permute-done.11.high_ref
  65.6 1.4 %shard_map.90.product_ref = f32[1152,128]{1,0:T(8,128)S(1)} custom-call(s32[12]{0:T(128)S(1)} %concatenate.9.where, bf16[1152,128]{1,0:T(8,128)(2,1)S(1)} %collective-permute-done.8.low_ref.x_ref, bf16[1152,128]{1,0:T(8,128)(2,1)S(1)} %collective-permute-done.11.high_ref, bf16[576,1152]{1,0:T(8,128)(2,1)S(1)} %bitcast.25, ...), custom_call_target="tpu_custom_call" | custom-call | flops 339738624 | bytes 3833904 | tf_op jit(solution)/shard_map/pallas_call | solution.py:30
  67.0 0.0 collective-permute-done.13.low_skip_ref
  67.0 6.9 %collective-permute-done.12.skip_ref = bf16[1152,128]{1,0:T(8,128)(2,1)S(1)} collective-permute-done((bf16[1152,128]{1,0:T(8,128)(2,1)S(1)}, bf16[1152,128]{1,0:T(8,128)(2,1)S(1)}, u32[]{:S(2)}, u32[]{:S(2)}) %collective-permute-start.12) | collective-permute-done | bytes 294944 | tf_op jit(solution)/shard_map/ppermute | solution.py:298
  73.8 0.9 %shard_map.92 = (bf16[1152,128]{1,0:T(8,128)(2,1)S(1)}, f32[1152,128]{1,0:T(8,128)S(1)}) custom-call(s32[12]{0:T(128)S(1)} %concatenate.9.where, bf16[1152,128]{1,0:T(8,128)(2,1)S(1)} %get-tuple-element.35.x_ref.fresh_ref, bf16[1152,128]{1,0:T(8,128)(2,1)S(1)} %collective-permute-done.8.low_ref.x_ref, f32[1152,128]{1,0:T(8,128)S(1)} %shard_map.90.product_ref, ...), custom_call_target="tpu_custom_call" | custom-call | flops 1769472 | bytes 2949168 | tf_op jit(solution)/shard_map/pallas_call | solution.py:30
  74.7 1.8 %collective-permute-start.14 = (bf16[1152,128]{1,0:T(8,128)(2,1)S(1)}, bf16[1152,128]{1,0:T(8,128)(2,1)S(1)}, u32[]{:S(2)}, u32[]{:S(2)}) collective-permute-start(bf16[1152,128]{1,0:T(8,128)(2,1)S(1)} %get-tuple-element.43.own_ref), channel_id=1, source_target_pairs={{0,1},{1,0},{2,3},{3,2},{4,5},{5,4},{6,7},{7,6},{8,9},{9,8},{10,11... | collective-permute-start | bytes 884744 | tf_op jit(solution)/shard_map/ppermute | solution.py:295
  76.5 1.2 %collective-permute-done.14.other_ref = bf16[1152,128]{1,0:T(8,128)(2,1)S(1)} collective-permute-done((bf16[1152,128]{1,0:T(8,128)(2,1)S(1)}, bf16[1152,128]{1,0:T(8,128)(2,1)S(1)}, u32[]{:S(2)}, u32[]{:S(2)}) %collective-permute-start.14) | collective-permute-done | bytes 294944 | tf_op jit(solution)/shard_map/ppermute | solution.py:295
  77.7 2.9 %shard_map.93 = (f32[576,128]{1,0:T(8,128)S(1)}, f32[576,128]{1,0:T(8,128)S(1)}) custom-call(s32[12]{0:T(128)S(1)} %concatenate.9.where, bf16[1152,128]{1,0:T(8,128)(2,1)S(1)} %get-tuple-element.43.own_ref, bf16[1152,128]{1,0:T(8,128)(2,1)S(1)} %collective-permute-done.14.other_ref, f32[1152,128]{1,0:T(8,128)S(1)} %get-tuple-element.44.hidden_ref, ...), custom_call_target="tpu_custom_call" | custom-call | flops 2038431744 | bytes 7372848 | tf_op jit(solution)/shard_map/pallas_call | solution.py:30
  80.7 0.4 collective-permute-start.15
  81.1 1.2 %collective-permute-done.15 = f32[576,128]{1,0:T(8,128)S(1)} collective-permute-done((f32[576,128]{1,0:T(8,128)S(1)}, f32[576,128]{1,0:T(8,128)S(1)}, u32[]{:S(2)}, u32[]{:S(2)}) %collective-permute-start.15) | collective-permute-done | bytes 294944 | tf_op jit(solution)/shard_map/ppermute | solution.py:295
  82.3 0.9 %fusion = f32[1,256,576]{1,2,0:T(8,128)} fusion(f32[576,128]{1,0:T(8,128)S(1)} %collective-permute-done.15, f32[576,128]{1,0:T(8,128)S(1)} %get-tuple-element.45, pred[]{:T(512)S(6)} %eq.3), kind=kLoop, calls=%fused_computation.1 | loop fusion | flops 442368 | bytes 1179649 | tf_op jit(solution)/shard_map/broadcast_in_dim | solution.py:427
Async XLA Ops:
  0.0 10.1 %collective-permute-start.1 = (bf16[3,288,1152]{2,1,0:T(8,128)(2,1)}, bf16[3,288,1152]{2,1,0:T(8,128)(2,1)S(1)}, u32[]{:S(2)}, u32[]{:S(2)}) collective-permute-start(bf16[3,288,1152]{2,1,0:T(8,128)(2,1)} %bitcast.32), channel_id=1, source_target_pairs={{0,1},{1,0},{2,3},{3,2},{4,5},{5,4},{6,7},{7,6},{8,9},{9,8},{10,11... | collective-permute-start | bytes 5971976 | tf_op jit(solution)/shard_map/ppermute | solution.py:295
  0.7 9.4 %collective-permute-start.2 = (bf16[288,1152]{1,0:T(8,128)(2,1)}, bf16[288,1152]{1,0:T(8,128)(2,1)S(1)}, u32[]{:S(2)}, u32[]{:S(2)}) collective-permute-start(bf16[288,1152]{1,0:T(8,128)(2,1)} %bitcast.37), channel_id=1, source_target_pairs={{0,1},{1,0},{2,3},{3,2},{4,5},{5,4},{6,7},{7,6},{8,9},{9,8},{10,11... | collective-permute-start | bytes 1990664 | tf_op jit(solution)/shard_map/ppermute | solution.py:295
  0.7 5.2 %collective-permute-start = (bf16[2,576,128]{2,1,0:T(8,128)(2,1)}, bf16[2,576,128]{2,1,0:T(8,128)(2,1)S(1)}, u32[]{:S(2)}, u32[]{:S(2)}) collective-permute-start(bf16[2,576,128]{2,1,0:T(8,128)(2,1)} %bitcast.27), channel_id=1, source_target_pairs={{0,1},{1,0},{2,3},{3,2},{4,5},{5,4},{6,7},{7,6},{8,9},{9,8},{10,11... | collective-permute-start | bytes 884744 | tf_op jit(solution)/shard_map/ppermute | solution.py:295
  5.9 1.1 %copy-start.1 = (bf16[1,256,1152]{2,1,0:T(8,128)(2,1)S(1)}, bf16[1,256,1152]{2,1,0:T(8,128)(2,1)}, u32[]{:S(2)}) copy-start(bf16[1,256,1152]{2,1,0:T(8,128)(2,1)} %param.8) | copy-start | bytes 1769476
  7.0 1.0 %copy-start.2 = (bf16[1,128,2,576]{1,3,2,0:T(8,128)(2,1)S(1)}, bf16[1,128,2,576]{1,3,2,0:T(8,128)(2,1)}, u32[]{:S(2)}) copy-start(bf16[1,128,2,576]{1,3,2,0:T(8,128)(2,1)} %param.13) | copy-start | bytes 884740
  10.1 1.6 %copy-start.4 = (bf16[1,3,1152,288]{2,3,1,0:T(8,128)(2,1)S(1)}, bf16[1,3,1152,288]{2,3,1,0:T(8,128)(2,1)}, u32[]{:S(2)}) copy-start(bf16[1,3,1152,288]{2,3,1,0:T(8,128)(2,1)} %param.11) | copy-start | bytes 5971972
  11.6 1.1 %copy-start.6 = (bf16[1,288,1152]{2,1,0:T(8,128)(2,1)S(1)}, bf16[1,288,1152]{2,1,0:T(8,128)(2,1)}, u32[]{:S(2)}) copy-start(bf16[1,288,1152]{2,1,0:T(8,128)(2,1)} %param.12) | copy-start | bytes 1990660
  12.7 5.0 %copy-start = (bf16[1,1152,576]{1,2,0:T(8,128)(2,1)S(1)}, bf16[1,1152,576]{1,2,0:T(8,128)(2,1)}, u32[]{:S(2)}) copy-start(bf16[1,1152,576]{1,2,0:T(8,128)(2,1)} %param.10) | copy-start | bytes 3981316
  12.7 6.9 %copy-start.3 = (bf16[2,1,64,1152]{3,2,1,0:T(8,128)(2,1)S(1)}, bf16[2,1,64,1152]{3,2,1,0:T(8,128)(2,1)}, u32[]{:S(2)}) copy-start(bf16[2,1,64,1152]{3,2,1,0:T(8,128)(2,1)} %param.9) | copy-start | bytes 884740
  17.7 15.6 %copy-start.5 = (bf16[1,3,1152,288]{2,3,1,0:T(8,128)(2,1)S(1)}, bf16[1,3,1152,288]{2,3,1,0:T(8,128)(2,1)}, u32[]{:S(2)}) copy-start(bf16[1,3,1152,288]{2,3,1,0:T(8,128)(2,1)} %param.11) | copy-start | bytes 5971972
  17.7 10.9 %collective-permute-start.4 = (bf16[576,1152]{1,0:T(8,128)(2,1)S(1)}, bf16[576,1152]{1,0:T(8,128)(2,1)S(1)}, u32[]{:S(2)}, u32[]{:S(2)}) collective-permute-start(bf16[576,1152]{1,0:T(8,128)(2,1)S(1)} %bitcast.21), channel_id=1, source_target_pairs={{0,1},{1,0},{2,3},{3,2},{4,5},{5,4},{6,7},{7,6},{8,9},{9,8},{10,11... | collective-permute-start | bytes 3981320 | tf_op jit(solution)/shard_map/ppermute | solution.py:295
  18.2 10.5 %collective-permute-start.3 = (bf16[1152,128]{1,0:T(8,128)(2,1)S(1)}, bf16[1152,128]{1,0:T(8,128)(2,1)S(1)}, u32[]{:S(2)}, u32[]{:S(2)}) collective-permute-start(bf16[1152,128]{1,0:T(8,128)(2,1)S(1)} %get-tuple-element.30), channel_id=1, source_target_pairs={{0,4},{4,8},{1,5},{5,9},{2,6},{6,10},{3,7},{7,11},{16,20},{20,24},... | collective-permute-start | bytes 884744 | tf_op jit(solution)/shard_map/ppermute | solution.py:298
  19.6 10.7 %collective-permute-start.5 = (bf16[2,64,1152]{2,1,0:T(8,128)(2,1)S(1)}, bf16[2,64,1152]{2,1,0:T(8,128)(2,1)S(1)}, u32[]{:S(2)}, u32[]{:S(2)}) collective-permute-start(bf16[2,64,1152]{2,1,0:T(8,128)(2,1)S(1)} %bitcast.29), channel_id=1, source_target_pairs={{9,1},{11,3},{25,17},{27,19}} | collective-permute-start | bytes 884744 | tf_op jit(solution)/shard_map/ppermute | solution.py:380
  23.5 6.8 %collective-permute-start.6 = (bf16[2,64,1152]{2,1,0:T(8,128)(2,1)S(1)}, bf16[2,64,1152]{2,1,0:T(8,128)(2,1)S(1)}, u32[]{:S(2)}, u32[]{:S(2)}) collective-permute-start(bf16[2,64,1152]{2,1,0:T(8,128)(2,1)S(1)} %bitcast.30), channel_id=1, source_target_pairs={{4,0},{13,1},{6,2},{15,3},{20,16},{29,17},{22,18},{31,19}} | collective-permute-start | bytes 884744 | tf_op jit(solution)/shard_map/ppermute | solution.py:380
  31.2 2.0 %collective-permute-start.7 = (bf16[1152,128]{1,0:T(8,128)(2,1)S(1)}, bf16[1152,128]{1,0:T(8,128)(2,1)S(1)}, u32[]{:S(2)}, u32[]{:S(2)}) collective-permute-start(bf16[1152,128]{1,0:T(8,128)(2,1)S(1)} %get-tuple-element.36.own_ref), channel_id=1, source_target_pairs={{0,1},{1,0},{2,3},{3,2},{4,5},{5,4},{6,7},{7,6},{8,9},{9,8},{10,11... | collective-permute-start | bytes 884744 | tf_op jit(solution)/shard_map/ppermute | solution.py:295
  32.0 12.6 %collective-permute-start.9 = (bf16[1152,128]{1,0:T(8,128)(2,1)S(1)}, bf16[1152,128]{1,0:T(8,128)(2,1)S(1)}, u32[]{:S(2)}, u32[]{:S(2)}) collective-permute-start(bf16[1152,128]{1,0:T(8,128)(2,1)S(1)} %get-tuple-element.33.order_ref), channel_id=1, source_target_pairs={{4,8},{5,9},{6,10},{7,11},{20,24},{21,25},{22,26},{23,27}} | collective-permute-start | bytes 884744 | tf_op jit(solution)/shard_map/ppermute | solution.py:298
  45.5 2.8 %collective-permute-start.10 = (bf16[1152,128]{1,0:T(8,128)(2,1)S(1)}, bf16[1152,128]{1,0:T(8,128)(2,1)S(1)}, u32[]{:S(2)}, u32[]{:S(2)}) collective-permute-start(bf16[1152,128]{1,0:T(8,128)(2,1)S(1)} %get-tuple-element.41.own_ref), channel_id=1, source_target_pairs={{0,1},{1,0},{2,3},{3,2},{4,5},{5,4},{6,7},{7,6},{8,9},{9,8},{10,11... | collective-permute-start | bytes 884744 | tf_op jit(solution)/shard_map/ppermute | solution.py:295
  46.1 16.7 %collective-permute-start.8 = (bf16[1152,128]{1,0:T(8,128)(2,1)S(1)}, bf16[1152,128]{1,0:T(8,128)(2,1)S(1)}, u32[]{:S(2)}, u32[]{:S(2)}) collective-permute-start(bf16[1152,128]{1,0:T(8,128)(2,1)S(1)} %shard_map.86.order_ref), channel_id=1, source_target_pairs={{0,4},{4,8},{1,5},{5,9},{2,6},{6,10},{3,7},{7,11},{16,20},{20,24},... | collective-permute-start | bytes 884744 | tf_op jit(solution)/shard_map/ppermute | solution.py:298
  47.4 19.5 %collective-permute-start.13 = (bf16[1152,128]{1,0:T(8,128)(2,1)S(1)}, bf16[1152,128]{1,0:T(8,128)(2,1)S(1)}, u32[]{:S(2)}, u32[]{:S(2)}) collective-permute-start(bf16[1152,128]{1,0:T(8,128)(2,1)S(1)} %shard_map.87.order_ref), channel_id=1, source_target_pairs={{0,12},{1,13},{2,14},{3,15},{16,28},{17,29},{18,30},{19,31}} | collective-permute-start | bytes 884744 | tf_op jit(solution)/shard_map/ppermute | solution.py:298
  51.2 14.3 %collective-permute-start.11 = (bf16[1152,128]{1,0:T(8,128)(2,1)S(1)}, bf16[1152,128]{1,0:T(8,128)(2,1)S(1)}, u32[]{:S(2)}, u32[]{:S(2)}) collective-permute-start(bf16[1152,128]{1,0:T(8,128)(2,1)S(1)} %shard_map.89.order_ref), channel_id=1, source_target_pairs={{8,12},{9,13},{10,14},{11,15},{24,28},{25,29},{26,30},{27,31}} | collective-permute-start | bytes 884744 | tf_op jit(solution)/shard_map/ppermute | solution.py:298
  64.3 9.6 %collective-permute-start.12 = (bf16[1152,128]{1,0:T(8,128)(2,1)S(1)}, bf16[1152,128]{1,0:T(8,128)(2,1)S(1)}, u32[]{:S(2)}, u32[]{:S(2)}) collective-permute-start(bf16[1152,128]{1,0:T(8,128)(2,1)S(1)} %shard_map.91), channel_id=1, source_target_pairs={{4,8},{5,9},{6,10},{7,11},{20,24},{21,25},{22,26},{23,27}} | collective-permute-start | bytes 884744 | tf_op jit(solution)/shard_map/ppermute | solution.py:298
  74.7 3.0 %collective-permute-start.14 = (bf16[1152,128]{1,0:T(8,128)(2,1)S(1)}, bf16[1152,128]{1,0:T(8,128)(2,1)S(1)}, u32[]{:S(2)}, u32[]{:S(2)}) collective-permute-start(bf16[1152,128]{1,0:T(8,128)(2,1)S(1)} %get-tuple-element.43.own_ref), channel_id=1, source_target_pairs={{0,1},{1,0},{2,3},{3,2},{4,5},{5,4},{6,7},{7,6},{8,9},{9,8},{10,11... | collective-permute-start | bytes 884744 | tf_op jit(solution)/shard_map/ppermute | solution.py:295
  80.7 1.6 %collective-permute-start.15 = (f32[576,128]{1,0:T(8,128)S(1)}, f32[576,128]{1,0:T(8,128)S(1)}, u32[]{:S(2)}, u32[]{:S(2)}) collective-permute-start(f32[576,128]{1,0:T(8,128)S(1)} %get-tuple-element.46), channel_id=1, source_target_pairs={{0,1},{1,0},{2,3},{3,2},{4,5},{5,4},{6,7},{7,6},{8,9},{9,8},{10,11... | collective-permute-start | bytes 884744 | tf_op jit(solution)/shard_map/ppermute | solution.py:295
where the time goes:
time: 83.6 us; the launch traced here: 83.2 us
  waiting for transfers between devices  36.2 us (43%)
  Pallas kernels  23.2 us (28%)
  starting transfers between devices  17.3 us (21%)
  local copies, waits for them, and re-layouts  5.42 us (6%)
  other arithmetic  0.85 us (1%)
    ppermute x6, waiting for transfers between devices, moved(): return lax.ppermute(value, 'section', pairs)  29.5 us
    pallas_call x12, Pallas kernels, call(): pl.pallas_call(body, out_shape=tuple(outs), in_specs=in_specs, out_specs=...  23.2 us
    ppermute x6, starting transfers between devices, moved(): return lax.ppermute(value, 'section', pairs)  7.43 us
    ppermute x8, waiting for transfers between devices, swapped(): return lax.ppermute(value, 'tensor', [(0, 1), (1, 0)])  6.39 us
    ppermute x8, starting transfers between devices, swapped(): return lax.ppermute(value, 'tensor', [(0, 1), (1, 0)])  5.28 us
    unnamed x14, local copies, waits for them, and re-layouts  4.68 us
    ppermute x2, starting transfers between devices, relayed(): blocks.append(lax.ppermute(fresh_block, ('section', 'tensor'), pairs))  4.58 us
  transfers between devices with their start and end apart: 16, of which 8 were waited for; matrix products, arithmetic and copies ran while one was open for 1% of the time, Pallas kernels for 15%

commit v1 on v0

--- a/solution.py
+++ b/solution.py
@@ -22,18 +22,20 @@
 TICK_LANES = 32
 CHUNK = 96
 PLACES = 3
-FULL = 24 << 20
-
-
-def call(body, outs, in_specs, flops, args, scratch=(), limit=24 << 20):
+
+
+def call(body, outs, in_specs, flops, args, scratch=()):
     moved = sum(math.prod(a.shape) * a.dtype.itemsize for a in (*args, *outs))
+    args = [
+        pltpu.with_memory_space_constraint(a, pltpu.HBM) if spec is HBM else a for a, spec in zip(args, in_specs)
+    ]
     return pl.pallas_call(
         body,
         out_shape=tuple(outs),
         in_specs=in_specs,
         out_specs=tuple(VMEM for _ in outs),
         scratch_shapes=list(scratch),
-        compiler_params=pltpu.CompilerParams(vmem_limit_bytes=limit),
+        compiler_params=pltpu.CompilerParams(vmem_limit_bytes=24 << 20),
         cost_estimate=pl.CostEstimate(flops=flops, bytes_accessed=moved, transcendentals=0),
     )(*args)
 
@@ -85,14 +87,14 @@
 
 
 def first_kernel(
-    where, mod_own_hbm, mod_other_hbm, x_hbm,
+    where, mod_own_hbm, x_hbm, mod_other,
     scale_ref, gate_ref, own_ref, other_ref, hidden_ref,
-    mod_own, mod_other, x_ref, turned, sems,
+    mod_own, x_ref, turned, sems,
 ):
     copies = [
         pltpu.make_async_copy(source, target, sems.at[index])
         for index, (source, target) in enumerate(
-            ((mod_own_hbm, mod_own), (mod_other_hbm, mod_other), (x_hbm, x_ref))
+            ((mod_own_hbm, mod_own), (x_hbm, x_ref))
         )
     ]
     for copy in copies:
@@ -137,7 +139,7 @@
             normalise(lambda rows: turned[rows, columns], storing(other_ref), scale_ref, 0)
 
 
-def norm_kernel(tick, where, arrived_ref, scale_ref, order_ref, *refs):
+def ahead_norm_kernel(tick, where, scale_ref, *refs):
     *blocks, current_ref, mixed_ref, later_ref = refs
 
     @pl.when(where[2] == 0)
@@ -148,37 +150,48 @@
             )
             rows = [head] + [ref[index].astype(jnp.float32) for ref in blocks[2:]]
             target[...] = jnp.transpose(jnp.concatenate(rows, axis=0), (1, 0)).astype(jnp.bfloat16)
-
-    @pl.when(where[2] != 0)
-    def _():
-        current_ref[...] = arrived_ref[...]
-
-    normalise(lambda rows: current_ref[rows, :].astype(jnp.float32), storing(mixed_ref), scale_ref, tick)
-
-
-def product_kernel(where, x_ref, own_ref, other_ref, *results):
-    half = own_ref.shape[0]
-    for ref, rows in zip((own_ref, other_ref), halves(where[0], half)):
-        product = jnp.dot(ref[...], x_ref[...], preferred_element_type=jnp.float32)
+        normalise(lambda rows: current_ref[rows, :].astype(jnp.float32), storing(mixed_ref), scale_ref, tick)
+
+
+def norm_kernel(tick, where, x_ref, scale_ref, order_ref, mixed_ref):
+    normalise(lambda rows: x_ref[rows, :].astype(jnp.float32), storing(mixed_ref), scale_ref, tick)
+
+
+def multiply(where, value, own_ref, other_ref, results):
+    for ref, rows in zip((own_ref, other_ref), halves(where[0], own_ref.shape[0])):
+        product = jnp.dot(ref[...], value, preferred_element_type=jnp.float32)
         for result in results:
             result[rows, :] = product.astype(result.dtype)
 
 
+def product_kernel(where, x_ref, own_ref, other_ref, *results):
+    multiply(where, x_ref[...], own_ref, other_ref, results)
+
+
+def outgoing_kernel(where, x_ref, ahead_ref, own_ref, other_ref, order_ref, wide_ref, narrow_ref):
+    @pl.when(where[2] == 0)
+    def _():
+        narrow_ref[...] = ahead_ref[...]
+
+    @pl.when(where[2] != 0)
+    def _():
+        multiply(where, x_ref[...], own_ref, other_ref, (wide_ref, narrow_ref))
+
+
 def lowest_kernel(where, x_ref, own_ref, other_ref, order_ref, narrow_ref):
     @pl.when(where[2] == 0)
     def _():
-        product_kernel(where, x_ref, own_ref, other_ref, narrow_ref)
-
-
-def skip_kernel(where, x_ref, own_ref, other_ref, order_ref, narrow_ref):
-    product_kernel(where, x_ref, own_ref, other_ref, narrow_ref)
-
-
-def chosen_kernel(middle, where, low_ref, high_ref, own_ref, other_ref, wide_ref):
-    half = own_ref.shape[0]
-    value = jnp.where(where[2] == middle, low_ref[...], high_ref[...])
-    for ref, rows in zip((own_ref, other_ref), halves(where[0], half)):
-        wide_ref[rows, :] = jnp.dot(ref[...], value, preferred_element_type=jnp.float32)
+        multiply(where, x_ref[...], own_ref, other_ref, (narrow_ref,))
+
+
+def skip_kernel(where, low_ref, ahead_ref, own_ref, other_ref, order_ref, narrow_ref):
+    @pl.when(where[2] == 1)
+    def _():
+        multiply(where, ahead_ref[...], own_ref, other_ref, (narrow_ref,))
+
+    @pl.when((where[1] == 0) & (where[2] > 1))
+    def _():
+        multiply(where, low_ref[...], own_ref, other_ref, (narrow_ref,))
 
 
 def joined_kernel(tick, where, product_ref, skip_ref, scale_ref, order_ref, mixed_ref, hidden_ref):
@@ -189,41 +202,55 @@
 
 
 def last_joined_kernel(
-    tick, last, where, fresh_ref, low_ref, product_ref, skip_ref, low_skip_ref, scale_ref, mixed_ref, hidden_ref
+    tick, middle, last, where, fresh_ref, ahead_ref, low_ref, high_ref, skip_ref, low_skip_ref, own_ref, other_ref,
+    scale_ref, mixed_ref, hidden_ref,
 ):
-    @pl.when((where[1] == 1) & (where[2] == last))
-    def _():
-        hidden_ref[...] = product_ref[...] + low_skip_ref[...].astype(jnp.float32)
-
-    @pl.when((where[1] == 1) & (where[2] != last))
-    def _():
-        hidden_ref[...] = product_ref[...] + skip_ref[...].astype(jnp.float32)
-
-    @pl.when((where[1] == 0) & (where[2] == 0))
-    def _():
-        hidden_ref[...] = fresh_ref[...].astype(jnp.float32)
-
-    @pl.when((where[1] == 0) & (where[2] != 0))
-    def _():
-        hidden_ref[...] = low_ref[...].astype(jnp.float32)
+    @pl.when(where[1] == 1)
+    def _():
+        value = jnp.where(where[2] == middle, low_ref[...], high_ref[...])
+        multiply(where, value, own_ref, other_ref, (hidden_ref,))
+
+    for here, source in (
+        (where[2] == 0, fresh_ref),
+        (where[2] == 1, ahead_ref),
+        ((where[1] == 0) & (where[2] > 1), low_ref),
+    ):
+
+        @pl.when(here)
+        def _():
+            hidden_ref[...] = source[...].astype(jnp.float32)
+
+    for here, source in (
+        ((where[1] == 1) & (where[2] == last), low_skip_ref),
+        ((where[1] == 1) & (where[2] != last), skip_ref),
+    ):
+
+        @pl.when(here)
+        def _():
+            hidden_ref[...] += source[...].astype(jnp.float32)
 
     normalise(lambda rows: hidden_ref[rows, :], storing(mixed_ref), scale_ref, tick)
 
 
+def ahead_block_kernel(tick, where, *refs):
+    @pl.when(where[2] == 0)
+    def _():
+        block_kernel(tick, "middle", where, *refs)
+
+
 def block_kernel(
-    tick, stage, where, own_ref, other_ref, hidden_ref, gate_ref, qkv_own, qkv_other, out_own, out_other, *rest
+    tick, stage, where, order_ref, own_ref, other_ref, hidden_ref, gate_ref, qkv_own, qkv_other, out_own, out_other,
+    *rest,
 ):
     if stage == "first":
-        *results, scores, raised, attended, held_a, held_b, raw_a, raw_b, sems = rest
+        *results, scores, raised, attended, held, raw, sems = rest
         copies = [
             pltpu.make_async_copy(source, target, sems.at[index])
-            for index, (source, target) in enumerate(
-                ((qkv_own, held_a), (qkv_other, held_b), (out_own, raw_a), (out_other, raw_b))
-            )
+            for index, (source, target) in enumerate(((qkv_own, held), (out_own, raw)))
         ]
         for copy in copies:
             copy.start()
-        projections, turned = (held_a, held_b), results[1:]
+        projections, turned = (qkv_other, held), results[2:0:-1]
     else:
         *results, scores, raised, attended = rest
         projections, turned = (qkv_own, qkv_other), (out_own, out_other)
@@ -233,8 +260,8 @@
     heads = head_cols // DH
     values = []
     for group, ref in enumerate(projections):
-        if stage == "first":
-            copies[group].wait()
+        if stage == "first" and group == 1:
+            copies[0].wait()
         query = jnp.dot(ref[0], own, preferred_element_type=jnp.float32).astype(jnp.bfloat16)
         key = jnp.dot(ref[1], both, preferred_element_type=jnp.float32).astype(jnp.bfloat16)
         values.append(jnp.dot(ref[2], both, preferred_element_type=jnp.float32).astype(jnp.bfloat16))
@@ -244,8 +271,8 @@
                 key[rows], query[rows], (((0,), (0,)), ((), ())), preferred_element_type=jnp.float32
             ) * (1.0 / math.sqrt(DH))
     if stage == "first":
-        for index, (source, target) in enumerate(zip((raw_a, raw_b), turned)):
-            copies[2 + index].wait()
+        copies[1].wait()
+        for source, target in zip((out_other, raw), turned):
             target[...] = jnp.transpose(source[...].astype(jnp.float32), (1, 0)).astype(jnp.bfloat16)
     weights = []
     for head in range(2 * heads):
@@ -314,19 +341,17 @@
     block_flops = 6 * product_flops
 
     scale, gate, own, other, hidden = call(
-        first_kernel, [lanes, lanes, narrow, narrow, narrow], [SMEM] + [HBM] * 3, 4 * norm_flops,
-        (where, mod_own, mod_other, inflow[0]),
+        first_kernel, [lanes, lanes, narrow, narrow, narrow], [SMEM, HBM, HBM, VMEM], 4 * norm_flops,
+        (where, mod_own, inflow[0], mod_other),
         [
-            pltpu.VMEM(mod_own.shape, jnp.bfloat16),
             pltpu.VMEM(mod_own.shape, jnp.bfloat16),
             pltpu.VMEM((row_count, width), jnp.bfloat16),
             pltpu.VMEM((width, row_count), jnp.float32),
-            pltpu.SemaphoreType.DMA((3,)),
+            pltpu.SemaphoreType.DMA((2,)),
         ],
-        FULL,
-    )
-
-    def attention(own, other, hidden, outs, tick, stage):
+    )
+
+    def attention(own, other, hidden, outs, tick, stage, order):
         results = [narrow]
         count = 2 * head_cols // DH
         scratch = [
@@ -337,18 +362,24 @@
         weights = [VMEM] * 4
         if stage == "first":
             results = [narrow, turned, turned]
-            weights = [HBM] * 4
-            scratch += [pltpu.VMEM(qkv_own.shape, jnp.bfloat16)] * 2
-            scratch += [pltpu.VMEM(out_own.shape, jnp.bfloat16)] * 2
-            scratch += [pltpu.SemaphoreType.DMA((4,))]
+            weights = [HBM, VMEM, HBM, VMEM]
+            scratch += [pltpu.VMEM(qkv_own.shape, jnp.bfloat16), pltpu.VMEM(out_own.shape, jnp.bfloat16)]
+            scratch += [pltpu.SemaphoreType.DMA((2,))]
         if stage == "last":
             results = [like((half, tokens), jnp.float32)] * 2
             scratch = [pltpu.VMEM((width, tokens), jnp.float32)] + scratch
         return call(
-            functools.partial(block_kernel, tick, stage), results, [SMEM] + [VMEM] * 4 + weights, block_flops,
-            (where, own, other, hidden, gate, qkv_own, qkv_other, *outs), scratch,
-            FULL if stage == "first" else 24 << 20,
+            functools.partial(ahead_block_kernel, tick) if stage == "ahead" else functools.partial(block_kernel, tick, stage),
+            results, [SMEM, ANY] + [VMEM] * 4 + weights, block_flops,
+            (where, order, own, other, hidden, gate, qkv_own, qkv_other, *outs), scratch,
         )
+
+    blocks = [fresh_rows[:, 0]]
+    for place in range(middle):
+        pairs = [
+            ((side * middle + place) * 2 + side, side) for side in range(2) if side or place
+        ]
+        blocks.append(lax.ppermute(fresh_rows[:, 0], ("section", "tensor"), pairs))
 
     early = middle <= sections - TICKS
     if early:
@@ -366,58 +397,57 @@
         own = jnp.where(upper, mixed, own)
         hidden = jnp.where(upper, joined, hidden.astype(jnp.float32))
         other = swapped(own)
-    settled, *outs = attention(own, other, hidden, (out_own, out_other), 0, "first")
-
+    settled, *outs = attention(own, other, hidden, (out_own, out_other), 0, "first", own)
     arrived = moved(settled, [(low, low + 1) for low in range(sections - 2)])
-    fresh_block, lin_source, _ = lax.optimization_barrier((fresh_rows[:, 0], lin_own, settled))
     if not early:
+        lin_source, _ = lax.optimization_barrier((lin_own, settled))
         lin_other = swapped(lin_source)
-    blocks = [fresh_block]
-    for place in range(middle):
-        pairs = [
-            ((side * middle + place) * 2 + side, side) for side in range(2) if side or place
-        ]
-        blocks.append(lax.ppermute(fresh_block, ("section", "tensor"), pairs))
-    products, outgoing = call(
-        product_kernel, [wide, narrow], [SMEM] + [VMEM] * 3, product_flops,
-        (where, arrived, lin_own, lin_other),
-    )
-    skip = moved(outgoing, [(low, sections - 1 - low) for low in range(1, middle)])
+
     current, own, later = call(
-        functools.partial(norm_kernel, 1), [narrow] * 3, [SMEM] + [VMEM] * 2 + [ANY] + [VMEM] * len(blocks), norm_flops,
-        (where, arrived, scale, outgoing, *blocks),
+        functools.partial(ahead_norm_kernel, 1), [narrow] * 3, [SMEM] + [VMEM] * (1 + len(blocks)), norm_flops,
+        (where, scale, *blocks),
     )
     other = swapped(own)
-    down = attention(own, other, current, outs, 1, "middle")[0]
-    arrived_low = moved(down, [(low, low + 1) for low in range(middle)])
+    ahead = attention(own, other, current, outs, 1, "ahead", own)[0]
     lowest = call(
         lowest_kernel, [narrow], [SMEM] + [VMEM] * 3 + [ANY], product_flops,
-        (where, later, lin_own, lin_other, down),
+        (where, later, lin_own, lin_other, ahead),
     )[0]
     low_skip = moved(lowest, [(0, sections - 1)])
+
+    products, outgoing = call(
+        outgoing_kernel, [wide, narrow], [SMEM] + [VMEM] * 4 + [ANY], product_flops,
+        (where, arrived, ahead, lin_own, lin_other, lowest),
+    )
+    skip = moved(outgoing, [(0, 1)] + [(low, sections - 1 - low) for low in range(1, middle)])
+    own = call(
+        functools.partial(norm_kernel, 1), [narrow], [SMEM] + [VMEM] * 2 + [ANY], norm_flops,
+        (where, arrived, scale, outgoing),
+    )[0]
+    other = swapped(own)
+    down = attention(own, other, arrived, outs, 1, "middle", own)[0]
+    arrived_low = moved(down, [(low, low + 1) for low in range(1, middle)])
+    ahead = skip
     own, hidden = call(
         functools.partial(joined_kernel, 1), [narrow, wide], [SMEM] + [VMEM] * 3 + [ANY], norm_flops,
-        (where, products, skip, scale, lowest),
+        (where, products, skip, scale, down),
     )
     other = swapped(own)
-    up = attention(own, other, hidden, outs, 1, "middle")[0]
-
-    arrived_high = moved(up, [(low, low + 1) for low in range(middle, sections - 1)])
     outgoing = call(
-        skip_kernel, [narrow], [SMEM] + [VMEM] * 3 + [ANY], product_flops,
-        (where, arrived_low, lin_own, lin_other, up),
+        skip_kernel, [narrow], [SMEM] + [VMEM] * 4 + [ANY], product_flops,
+        (where, arrived_low if middle > 2 else ahead, ahead, lin_own, lin_other, own),
     )[0]
     skip = moved(outgoing, [(low, sections - 1 - low) for low in range(1, middle)])
-    products = call(
-        functools.partial(chosen_kernel, middle), [wide], [SMEM] + [VMEM] * 4, product_flops,
-        (where, arrived_low, arrived_high, lin_own, lin_other),
-    )[0]
+    up = attention(own, other, hidden, outs, 1, "middle", outgoing)[0]
+
+    arrived_high = moved(up, [(low, low + 1) for low in range(middle, sections - 1)])
     own, hidden = call(
-        functools.partial(last_joined_kernel, 2, sections - 1), [narrow, wide], [SMEM] + [VMEM] * 6, norm_flops,
-        (where, later, arrived_low, products, skip, low_skip, scale),
+        functools.partial(last_joined_kernel, 2, middle, sections - 1), [narrow, wide],
+        [SMEM] + [VMEM] * 9, product_flops,
+        (where, later, ahead, arrived_low, arrived_high, skip, low_skip, lin_own, lin_other, scale),
     )
     other = swapped(own)
-    kept, sent = attention(own, other, hidden, outs, 2, "last")
+    kept, sent = attention(own, other, hidden, outs, 2, "last", own)
     received = swapped(sent)
     columns = jnp.where(
         core == 0,

time: 83.6 us -> 84.6 us (1.012)
  the two profiles are of different devices: /device:TPU:17 before, /device:TPU:23 now
where the time goes in v1:
time: 84.6 us; the launch traced here: 84.3 us
  waiting for transfers between devices  44.7 us (53%)
  Pallas kernels  23.8 us (28%)
  starting transfers between devices  14 us (17%)
  other arithmetic  0.86 us (1%)
    ppermute x6, waiting for transfers between devices, moved(): return lax.ppermute(value, 'section', pairs)  31.9 us
    pallas_call x13, Pallas kernels, call(): pl.pallas_call(body, out_shape=tuple(outs), in_specs=in_specs, out_specs=...  23.8 us
    ppermute x6, starting transfers between devices, moved(): return lax.ppermute(value, 'section', pairs)  7.31 us
    ppermute x9, waiting for transfers between devices, swapped(): return lax.ppermute(value, 'tensor', [(0, 1), (1, 0)])  6.66 us
    ppermute x2, waiting for transfers between devices, relayed(): blocks.append(lax.ppermute(fresh_rows[:, 0], ('section', 'tensor'), pairs))  6.15 us
    ppermute x9, starting transfers between devices, swapped(): return lax.ppermute(value, 'tensor', [(0, 1), (1, 0)])  3.99 us
    ppermute x2, starting transfers between devices, relayed(): blocks.append(lax.ppermute(fresh_rows[:, 0], ('section', 'tensor'), pairs))  2.65 us
  transfers between devices with their start and end apart: 17, of which 8 were waited for; matrix products, arithmetic and copies ran while one was open for 1% of the time, Pallas kernels for 13%

profile of v1, /device:TPU:23, one launch (start us, length us, event | category | flops | bytes accessed | tf_op | source)
XLA Modules:
  0.0 84.3 jit_solution(5141701936029331176)
XLA Ops:
  0.0 0.7 collective-permute-start.3
  0.7 0.0 collective-permute-start.4
  0.7 0.5 collective-permute-start
  1.2 0.7 concatenate.9.where
  1.9 4.0 %collective-permute-done.mod_other = bf16[2,576,128]{2,1,0:T(8,128)(2,1)S(1)} collective-permute-done((bf16[2,576,128]{2,1,0:T(8,128)(2,1)}, bf16[2,576,128]{2,1,0:T(8,128)(2,1)S(1)}, u32[]{:S(2)}, u32[]{:S(2)}) %collective-permute-start) | collective-permute-done | bytes 294944 | tf_op jit(solution)/shard_map/ppermute | solution.py:322
  5.9 2.9 %shard_map.82 = (bf16[1152,128]{1,0:T(8,128)(2,1)S(1)}, bf16[1152,128]{1,0:T(8,128)(2,1)S(1)}, bf16[1152,128]{1,0:T(8,128)(2,1)S(1)}, bf16[1152,128]{1,0:T(8,128)(2,1)S(1)}, bf16[1152,128]{1,0:T(8,128)(2,1)S(1)}) custom-call(s32[12]{0:T(128)S(1)} %concatenate.9.where, bf16[2,576,128]{2,1,0:T(8,128)(2,1)} %bitcast.37, bf16[256,1152]{1,0:T(8,128)(2,1)} %bitcast.35, ...), custom_call_target="tpu_custom_call" | custom-call | flops 7077888 | bytes 2654256 | tf_op jit(solution)/shard_map/pallas_call | solution.py:32
  8.8 0.0 collective-permute-done.4.out_other
  8.8 0.0 collective-permute-done.3.qkv_other.refs_6_
  8.8 0.0 copy-start
  8.8 0.0 copy-start.2
  8.8 0.0 copy-start.1
  8.8 5.0 %shard_map.84 = (bf16[1152,128]{1,0:T(8,128)(2,1)S(1)}, bf16[1152,288]{1,0:T(8,128)(2,1)S(1)}, bf16[1152,288]{1,0:T(8,128)(2,1)S(1)}) custom-call(s32[12]{0:T(128)S(1)} %concatenate.9.where, bf16[1152,128]{1,0:T(8,128)(2,1)S(1)} %get-tuple-element.27.order_ref.own_ref, bf16[1152,128]{1,0:T(8,128)(2,1)S(1)} %get-tuple-element.27.order_ref.own_ref, ...), custom_call_target="tpu_custom_call" | custom-call | flops 2038431744 | bytes 8405040 | tf_op jit(solution)/shard_map/pallas_call | solution.py:32
  13.9 0.0 copy-done
  13.9 0.4 collective-permute-start.7
  14.4 0.0 copy-done.2
  14.4 2.0 %collective-permute-start.1 = (bf16[2,64,1152]{2,1,0:T(8,128)(2,1)S(1)}, bf16[2,64,1152]{2,1,0:T(8,128)(2,1)S(1)}, u32[]{:S(2)}, u32[]{:S(2)}) collective-permute-start(bf16[2,64,1152]{2,1,0:T(8,128)(2,1)S(1)} %bitcast.32), channel_id=1, source_target_pairs={{9,1},{11,3},{25,17},{27,19}} | collective-permute-start | bytes 884744 | tf_op jit(solution)/shard_map/ppermute | solution.py:382
  16.3 0.7 collective-permute-start.2
  17.0 6.1 %collective-permute-done.1.refs_1_ = bf16[2,64,1152]{2,1,0:T(8,128)(2,1)S(1)} collective-permute-done((bf16[2,64,1152]{2,1,0:T(8,128)(2,1)S(1)}, bf16[2,64,1152]{2,1,0:T(8,128)(2,1)S(1)}, u32[]{:S(2)}, u32[]{:S(2)}) %collective-permute-start.1) | collective-permute-done | bytes 294944 | tf_op jit(solution)/shard_map/ppermute | solution.py:382
  23.2 0.0 collective-permute-done.2.refs_2_
  23.2 0.5 shard_map.83
  23.7 0.1 collective-permute-start.6
  23.8 1.3 %collective-permute-start.5 = (bf16[1152,128]{1,0:T(8,128)(2,1)S(1)}, bf16[1152,128]{1,0:T(8,128)(2,1)S(1)}, u32[]{:S(2)}, u32[]{:S(2)}) collective-permute-start(bf16[1152,128]{1,0:T(8,128)(2,1)S(1)} %get-tuple-element.31), channel_id=1, source_target_pairs={{0,4},{4,8},{1,5},{5,9},{2,6},{6,10},{3,7},{7,11},{16,20},{20,24},... | collective-permute-start | bytes 884744 | tf_op jit(solution)/shard_map/ppermute | solution.py:325
  25.1 0.3 collective-permute-done.6.refs_2_
  25.4 0.0 copy-done.1
  25.4 0.5 shard_map.85.order_ref.ahead_ref
  25.9 0.0 collective-permute-done.7.other_ref
  25.9 0.6 shard_map.86.order_ref
  26.5 11.2 %collective-permute-done.5.x_ref.hidden_ref = bf16[1152,128]{1,0:T(8,128)(2,1)S(1)} collective-permute-done((bf16[1152,128]{1,0:T(8,128)(2,1)S(1)}, bf16[1152,128]{1,0:T(8,128)(2,1)S(1)}, u32[]{:S(2)}, u32[]{:S(2)}) %collective-permute-start.5) | collective-permute-done | bytes 294944 | tf_op jit(solution)/shard_map/ppermute | solution.py:325
  37.7 1.4 %shard_map.87 = (f32[1152,128]{1,0:T(8,128)S(1)}, bf16[1152,128]{1,0:T(8,128)(2,1)S(1)}) custom-call(s32[12]{0:T(128)S(1)} %concatenate.9.where, bf16[1152,128]{1,0:T(8,128)(2,1)S(1)} %collective-permute-done.5.x_ref.hidden_ref, bf16[1152,128]{1,0:T(8,128)(2,1)S(1)} %shard_map.85.order_ref.ahead_ref, bf16[576,1152]{1,0:T(8,128)(2,1)S(1)} %bitcast.23, ...), custom_call_target="tpu_custom_call" | custom-call | flops 339738624 | bytes 4423728 | tf_op jit(solution)/shard_map/pallas_call | solution.py:32
  39.1 0.8 %shard_map.88.order_ref.own_ref = bf16[1152,128]{1,0:T(8,128)(2,1)S(1)} custom-call(s32[12]{0:T(128)S(1)} %concatenate.9.where, bf16[1152,128]{1,0:T(8,128)(2,1)S(1)} %collective-permute-done.5.x_ref.hidden_ref, bf16[1152,128]{1,0:T(8,128)(2,1)S(1)} %get-tuple-element.25.scale_ref, bf16[1152,128]{1,0:T(8,128)(2,1)S(1)} %get-tuple-element.37.order_ref), custom_call_target="tpu_custom_call" | custom-call | flops 1769472 | bytes 1179696 | tf_op jit(solution)/shard_map/pallas_call | solution.py:32
  40.0 0.7 collective-permute-start.9
  40.6 1.5 %collective-permute-start.8 = (bf16[1152,128]{1,0:T(8,128)(2,1)S(1)}, bf16[1152,128]{1,0:T(8,128)(2,1)S(1)}, u32[]{:S(2)}, u32[]{:S(2)}) collective-permute-start(bf16[1152,128]{1,0:T(8,128)(2,1)S(1)} %get-tuple-element.37.order_ref), channel_id=1, source_target_pairs={{0,4},{4,8},{1,5},{5,9},{2,6},{6,10},{3,7},{7,11},{16,20},{20,24},... | collective-permute-start | bytes 884744 | tf_op jit(solution)/shard_map/ppermute | solution.py:325
  42.1 0.0 collective-permute-done.9.other_ref
  42.1 2.9 %shard_map.89.order_ref = bf16[1152,128]{1,0:T(8,128)(2,1)S(1)} custom-call(s32[12]{0:T(128)S(1)} %concatenate.9.where, bf16[1152,128]{1,0:T(8,128)(2,1)S(1)} %shard_map.88.order_ref.own_ref, bf16[1152,128]{1,0:T(8,128)(2,1)S(1)} %shard_map.88.order_ref.own_ref, bf16[1152,128]{1,0:T(8,128)(2,1)S(1)} %collective-permute-done.9.other_ref, ...), custom_call_target="tpu_custom_call" | custom-call | flops 2038431744 | bytes 7077936 | tf_op jit(solution)/shard_map/pallas_call | solution.py:32
  45.1 6.9 %collective-permute-done.8.skip_ref.low_ref.ahead_ref = bf16[1152,128]{1,0:T(8,128)(2,1)S(1)} collective-permute-done((bf16[1152,128]{1,0:T(8,128)(2,1)S(1)}, bf16[1152,128]{1,0:T(8,128)(2,1)S(1)}, u32[]{:S(2)}, u32[]{:S(2)}) %collective-permute-start.8) | collective-permute-done | bytes 294944 | tf_op jit(solution)/shard_map/ppermute | solution.py:325
  52.0 0.9 %shard_map.90 = (bf16[1152,128]{1,0:T(8,128)(2,1)S(1)}, f32[1152,128]{1,0:T(8,128)S(1)}) custom-call(s32[12]{0:T(128)S(1)} %concatenate.9.where, f32[1152,128]{1,0:T(8,128)S(1)} %get-tuple-element.38.product_ref, bf16[1152,128]{1,0:T(8,128)(2,1)S(1)} %collective-permute-done.8.skip_ref.low_ref.ahead_ref, bf16[1152,128]{1,0:T(8,128)(2,1)S(1)} %get-tuple-element.25.scale_ref, ...), custom_call_target="tpu_custom_call" | custom-call | flops 1769472 | bytes 2359344 | tf_op jit(solution)/shard_map/pallas_call | solution.py:32
  52.8 0.7 collective-permute-start.11
  53.5 0.7 collective-permute-start.14
  54.2 1.3 %collective-permute-start.10 = (bf16[1152,128]{1,0:T(8,128)(2,1)S(1)}, bf16[1152,128]{1,0:T(8,128)(2,1)S(1)}, u32[]{:S(2)}, u32[]{:S(2)}) collective-permute-start(bf16[1152,128]{1,0:T(8,128)(2,1)S(1)} %shard_map.89.order_ref), channel_id=1, source_target_pairs={{4,8},{5,9},{6,10},{7,11},{20,24},{21,25},{22,26},{23,27}} | collective-permute-start | bytes 884744 | tf_op jit(solution)/shard_map/ppermute | solution.py:325
  55.5 0.6 shard_map.91.order_ref
  56.0 1.3 %collective-permute-start.13 = (bf16[1152,128]{1,0:T(8,128)(2,1)S(1)}, bf16[1152,128]{1,0:T(8,128)(2,1)S(1)}, u32[]{:S(2)}, u32[]{:S(2)}) collective-permute-start(bf16[1152,128]{1,0:T(8,128)(2,1)S(1)} %shard_map.91.order_ref), channel_id=1, source_target_pairs={{4,8},{5,9},{6,10},{7,11},{20,24},{21,25},{22,26},{23,27}} | collective-permute-start | bytes 884744 | tf_op jit(solution)/shard_map/ppermute | solution.py:325
  57.3 0.0 collective-permute-done.11.other_ref
  57.3 2.9 %shard_map.92 = bf16[1152,128]{1,0:T(8,128)(2,1)S(1)} custom-call(s32[12]{0:T(128)S(1)} %concatenate.9.where, bf16[1152,128]{1,0:T(8,128)(2,1)S(1)} %shard_map.91.order_ref, bf16[1152,128]{1,0:T(8,128)(2,1)S(1)} %get-tuple-element.39.order_ref.own_ref, bf16[1152,128]{1,0:T(8,128)(2,1)S(1)} %collective-permute-done.11.other_ref, ...), custom_call_target="tpu_custom_call" | custom-call | flops 2038431744 | bytes 7372848 | tf_op jit(solution)/shard_map/pallas_call | solution.py:32
  60.3 1.3 %collective-permute-start.12 = (bf16[1152,128]{1,0:T(8,128)(2,1)S(1)}, bf16[1152,128]{1,0:T(8,128)(2,1)S(1)}, u32[]{:S(2)}, u32[]{:S(2)}) collective-permute-start(bf16[1152,128]{1,0:T(8,128)(2,1)S(1)} %shard_map.92), channel_id=1, source_target_pairs={{8,12},{9,13},{10,14},{11,15},{24,28},{25,29},{26,30},{27,31}} | collective-permute-start | bytes 884744 | tf_op jit(solution)/shard_map/ppermute | solution.py:325
  61.6 0.0 collective-permute-done.14.low_skip_ref
  61.6 13.8 %collective-permute-done.13.skip_ref = bf16[1152,128]{1,0:T(8,128)(2,1)S(1)} collective-permute-done((bf16[1152,128]{1,0:T(8,128)(2,1)S(1)}, bf16[1152,128]{1,0:T(8,128)(2,1)S(1)}, u32[]{:S(2)}, u32[]{:S(2)}) %collective-permute-start.13) | collective-permute-done | bytes 294944 | tf_op jit(solution)/shard_map/ppermute | solution.py:325
  75.4 0.0 collective-permute-done.10.low_ref
  75.4 0.0 collective-permute-done.12.high_ref
  75.4 1.7 %shard_map.93 = (bf16[1152,128]{1,0:T(8,128)(2,1)S(1)}, f32[1152,128]{1,0:T(8,128)S(1)}) custom-call(s32[12]{0:T(128)S(1)} %concatenate.9.where, bf16[1152,128]{1,0:T(8,128)(2,1)S(1)} %get-tuple-element.26.x_ref.fresh_ref, bf16[1152,128]{1,0:T(8,128)(2,1)S(1)} %collective-permute-done.8.skip_ref.low_ref.ahead_ref, ...), custom_call_target="tpu_custom_call" | custom-call | flops 339738624 | bytes 5603376 | tf_op jit(solution)/shard_map/pallas_call | solution.py:32
  77.1 0.5 collective-permute-start.15
  77.6 1.2 %collective-permute-done.15.other_ref = bf16[1152,128]{1,0:T(8,128)(2,1)S(1)} collective-permute-done((bf16[1152,128]{1,0:T(8,128)(2,1)S(1)}, bf16[1152,128]{1,0:T(8,128)(2,1)S(1)}, u32[]{:S(2)}, u32[]{:S(2)}) %collective-permute-start.15) | collective-permute-done | bytes 294944 | tf_op jit(solution)/shard_map/ppermute | solution.py:322
  78.8 3.0 %shard_map.94 = (f32[576,128]{1,0:T(8,128)S(1)}, f32[576,128]{1,0:T(8,128)S(1)}) custom-call(s32[12]{0:T(128)S(1)} %concatenate.9.where, bf16[1152,128]{1,0:T(8,128)(2,1)S(1)} %get-tuple-element.41.order_ref.own_ref, bf16[1152,128]{1,0:T(8,128)(2,1)S(1)} %get-tuple-element.41.order_ref.own_ref, bf16[1152,128]{1,0:T(8,128)(2,1)S(1)} %collective-permute-done.15.other_ref, ...), custom_call_target="tpu_custom_call" | custom-call | flops 2038431744 | bytes 7667760 | tf_op jit(solution)/shard_map/pallas_call | solution.py:32
  81.8 0.4 collective-permute-start.16
  82.2 1.2 %collective-permute-done.16 = f32[576,128]{1,0:T(8,128)S(1)} collective-permute-done((f32[576,128]{1,0:T(8,128)S(1)}, f32[576,128]{1,0:T(8,128)S(1)}, u32[]{:S(2)}, u32[]{:S(2)}) %collective-permute-start.16) | collective-permute-done | bytes 294944 | tf_op jit(solution)/shard_map/ppermute | solution.py:322
  83.4 0.9 %fusion = f32[1,256,576]{1,2,0:T(8,128)} fusion(f32[576,128]{1,0:T(8,128)S(1)} %collective-permute-done.16, f32[576,128]{1,0:T(8,128)S(1)} %get-tuple-element.43, pred[]{:T(512)S(6)} %eq.3), kind=kLoop, calls=%fused_computation.1 | loop fusion | flops 442368 | bytes 1179649 | tf_op jit(solution)/shard_map/broadcast_in_dim | solution.py:457
Async XLA Ops:
  0.0 8.8 %collective-permute-start.3 = (bf16[3,288,1152]{2,1,0:T(8,128)(2,1)}, bf16[3,288,1152]{2,1,0:T(8,128)(2,1)S(1)}, u32[]{:S(2)}, u32[]{:S(2)}) collective-permute-start(bf16[3,288,1152]{2,1,0:T(8,128)(2,1)} %bitcast.26), channel_id=1, source_target_pairs={{0,1},{1,0},{2,3},{3,2},{4,5},{5,4},{6,7},{7,6},{8,9},{9,8},{10,11... | collective-permute-start | bytes 5971976 | tf_op jit(solution)/shard_map/ppermute | solution.py:322
  0.7 8.1 %collective-permute-start.4 = (bf16[288,1152]{1,0:T(8,128)(2,1)}, bf16[288,1152]{1,0:T(8,128)(2,1)S(1)}, u32[]{:S(2)}, u32[]{:S(2)}) collective-permute-start(bf16[288,1152]{1,0:T(8,128)(2,1)} %bitcast.40), channel_id=1, source_target_pairs={{0,1},{1,0},{2,3},{3,2},{4,5},{5,4},{6,7},{7,6},{8,9},{9,8},{10,11... | collective-permute-start | bytes 1990664 | tf_op jit(solution)/shard_map/ppermute | solution.py:322
  0.7 5.2 %collective-permute-start = (bf16[2,576,128]{2,1,0:T(8,128)(2,1)}, bf16[2,576,128]{2,1,0:T(8,128)(2,1)S(1)}, u32[]{:S(2)}, u32[]{:S(2)}) collective-permute-start(bf16[2,576,128]{2,1,0:T(8,128)(2,1)} %bitcast.36), channel_id=1, source_target_pairs={{0,1},{1,0},{2,3},{3,2},{4,5},{5,4},{6,7},{7,6},{8,9},{9,8},{10,11... | collective-permute-start | bytes 884744 | tf_op jit(solution)/shard_map/ppermute | solution.py:322
  8.8 5.1 %copy-start = (bf16[1,1152,576]{1,2,0:T(8,128)(2,1)S(1)}, bf16[1,1152,576]{1,2,0:T(8,128)(2,1)}, u32[]{:S(2)}) copy-start(bf16[1,1152,576]{1,2,0:T(8,128)(2,1)} %param.10) | copy-start | bytes 3981316
  8.8 5.5 %copy-start.2 = (bf16[2,1,64,1152]{3,2,1,0:T(8,128)(2,1)S(1)}, bf16[2,1,64,1152]{3,2,1,0:T(8,128)(2,1)}, u32[]{:S(2)}) copy-start(bf16[2,1,64,1152]{3,2,1,0:T(8,128)(2,1)} %param.9) | copy-start | bytes 884740
  8.8 16.5 %copy-start.1 = (bf16[1,3,1152,288]{2,3,1,0:T(8,128)(2,1)S(1)}, bf16[1,3,1152,288]{2,3,1,0:T(8,128)(2,1)}, u32[]{:S(2)}) copy-start(bf16[1,3,1152,288]{2,3,1,0:T(8,128)(2,1)} %param.11) | copy-start | bytes 5971972
  13.9 12.0 %collective-permute-start.7 = (bf16[576,1152]{1,0:T(8,128)(2,1)S(1)}, bf16[576,1152]{1,0:T(8,128)(2,1)S(1)}, u32[]{:S(2)}, u32[]{:S(2)}) collective-permute-start(bf16[576,1152]{1,0:T(8,128)(2,1)S(1)} %bitcast.21), channel_id=1, source_target_pairs={{0,1},{1,0},{2,3},{3,2},{4,5},{5,4},{6,7},{7,6},{8,9},{9,8},{10,11... | collective-permute-start | bytes 3981320 | tf_op jit(solution)/shard_map/ppermute | solution.py:322
  14.4 8.8 %collective-permute-start.1 = (bf16[2,64,1152]{2,1,0:T(8,128)(2,1)S(1)}, bf16[2,64,1152]{2,1,0:T(8,128)(2,1)S(1)}, u32[]{:S(2)}, u32[]{:S(2)}) collective-permute-start(bf16[2,64,1152]{2,1,0:T(8,128)(2,1)S(1)} %bitcast.32), channel_id=1, source_target_pairs={{9,1},{11,3},{25,17},{27,19}} | collective-permute-start | bytes 884744 | tf_op jit(solution)/shard_map/ppermute | solution.py:382
  16.3 6.8 %collective-permute-start.2 = (bf16[2,64,1152]{2,1,0:T(8,128)(2,1)S(1)}, bf16[2,64,1152]{2,1,0:T(8,128)(2,1)S(1)}, u32[]{:S(2)}, u32[]{:S(2)}) collective-permute-start(bf16[2,64,1152]{2,1,0:T(8,128)(2,1)S(1)} %bitcast.33), channel_id=1, source_target_pairs={{4,0},{13,1},{6,2},{15,3},{20,16},{29,17},{22,18},{31,19}} | collective-permute-start | bytes 884744 | tf_op jit(solution)/shard_map/ppermute | solution.py:382
  23.7 1.6 %collective-permute-start.6 = (bf16[1152,128]{1,0:T(8,128)(2,1)S(1)}, bf16[1152,128]{1,0:T(8,128)(2,1)S(1)}, u32[]{:S(2)}, u32[]{:S(2)}) collective-permute-start(bf16[1152,128]{1,0:T(8,128)(2,1)S(1)} %get-tuple-element.32.refs_0_.refs_1_), channel_id=1, source_target_pairs={{0,1},{1,0},{2,3},{3,2},{4,5},{5,4},{6,7},{7,6},{8,9},{9,8},{10,11... | collective-permute-start | bytes 884744 | tf_op jit(solution)/shard_map/ppermute | solution.py:322
  23.8 13.9 %collective-permute-start.5 = (bf16[1152,128]{1,0:T(8,128)(2,1)S(1)}, bf16[1152,128]{1,0:T(8,128)(2,1)S(1)}, u32[]{:S(2)}, u32[]{:S(2)}) collective-permute-start(bf16[1152,128]{1,0:T(8,128)(2,1)S(1)} %get-tuple-element.31), channel_id=1, source_target_pairs={{0,4},{4,8},{1,5},{5,9},{2,6},{6,10},{3,7},{7,11},{16,20},{20,24},... | collective-permute-start | bytes 884744 | tf_op jit(solution)/shard_map/ppermute | solution.py:325
  40.0 2.1 %collective-permute-start.9 = (bf16[1152,128]{1,0:T(8,128)(2,1)S(1)}, bf16[1152,128]{1,0:T(8,128)(2,1)S(1)}, u32[]{:S(2)}, u32[]{:S(2)}) collective-permute-start(bf16[1152,128]{1,0:T(8,128)(2,1)S(1)} %shard_map.88.order_ref.own_ref), channel_id=1, source_target_pairs={{0,1},{1,0},{2,3},{3,2},{4,5},{5,4},{6,7},{7,6},{8,9},{9,8},{10,11... | collective-permute-start | bytes 884744 | tf_op jit(solution)/shard_map/ppermute | solution.py:322
  40.6 11.3 %collective-permute-start.8 = (bf16[1152,128]{1,0:T(8,128)(2,1)S(1)}, bf16[1152,128]{1,0:T(8,128)(2,1)S(1)}, u32[]{:S(2)}, u32[]{:S(2)}) collective-permute-start(bf16[1152,128]{1,0:T(8,128)(2,1)S(1)} %get-tuple-element.37.order_ref), channel_id=1, source_target_pairs={{0,4},{4,8},{1,5},{5,9},{2,6},{6,10},{3,7},{7,11},{16,20},{20,24},... | collective-permute-start | bytes 884744 | tf_op jit(solution)/shard_map/ppermute | solution.py:325
  52.8 4.5 %collective-permute-start.11 = (bf16[1152,128]{1,0:T(8,128)(2,1)S(1)}, bf16[1152,128]{1,0:T(8,128)(2,1)S(1)}, u32[]{:S(2)}, u32[]{:S(2)}) collective-permute-start(bf16[1152,128]{1,0:T(8,128)(2,1)S(1)} %get-tuple-element.39.order_ref.own_ref), channel_id=1, source_target_pairs={{0,1},{1,0},{2,3},{3,2},{4,5},{5,4},{6,7},{7,6},{8,9},{9,8},{10,11... | collective-permute-start | bytes 884744 | tf_op jit(solution)/shard_map/ppermute | solution.py:322
  53.5 8.1 %collective-permute-start.14 = (bf16[1152,128]{1,0:T(8,128)(2,1)S(1)}, bf16[1152,128]{1,0:T(8,128)(2,1)S(1)}, u32[]{:S(2)}, u32[]{:S(2)}) collective-permute-start(bf16[1152,128]{1,0:T(8,128)(2,1)S(1)} %shard_map.86.order_ref), channel_id=1, source_target_pairs={{0,12},{1,13},{2,14},{3,15},{16,28},{17,29},{18,30},{19,31}} | collective-permute-start | bytes 884744 | tf_op jit(solution)/shard_map/ppermute | solution.py:325
  54.2 21.2 %collective-permute-start.10 = (bf16[1152,128]{1,0:T(8,128)(2,1)S(1)}, bf16[1152,128]{1,0:T(8,128)(2,1)S(1)}, u32[]{:S(2)}, u32[]{:S(2)}) collective-permute-start(bf16[1152,128]{1,0:T(8,128)(2,1)S(1)} %shard_map.89.order_ref), channel_id=1, source_target_pairs={{4,8},{5,9},{6,10},{7,11},{20,24},{21,25},{22,26},{23,27}} | collective-permute-start | bytes 884744 | tf_op jit(solution)/shard_map/ppermute | solution.py:325
  56.0 19.3 %collective-permute-start.13 = (bf16[1152,128]{1,0:T(8,128)(2,1)S(1)}, bf16[1152,128]{1,0:T(8,128)(2,1)S(1)}, u32[]{:S(2)}, u32[]{:S(2)}) collective-permute-start(bf16[1152,128]{1,0:T(8,128)(2,1)S(1)} %shard_map.91.order_ref), channel_id=1, source_target_pairs={{4,8},{5,9},{6,10},{7,11},{20,24},{21,25},{22,26},{23,27}} | collective-permute-start | bytes 884744 | tf_op jit(solution)/shard_map/ppermute | solution.py:325
  60.3 15.1 %collective-permute-start.12 = (bf16[1152,128]{1,0:T(8,128)(2,1)S(1)}, bf16[1152,128]{1,0:T(8,128)(2,1)S(1)}, u32[]{:S(2)}, u32[]{:S(2)}) collective-permute-start(bf16[1152,128]{1,0:T(8,128)(2,1)S(1)} %shard_map.92), channel_id=1, source_target_pairs={{8,12},{9,13},{10,14},{11,15},{24,28},{25,29},{26,30},{27,31}} | collective-permute-start | bytes 884744 | tf_op jit(solution)/shard_map/ppermute | solution.py:325
  77.1 1.7 %collective-permute-start.15 = (bf16[1152,128]{1,0:T(8,128)(2,1)S(1)}, bf16[1152,128]{1,0:T(8,128)(2,1)S(1)}, u32[]{:S(2)}, u32[]{:S(2)}) collective-permute-start(bf16[1152,128]{1,0:T(8,128)(2,1)S(1)} %get-tuple-element.41.order_ref.own_ref), channel_id=1, source_target_pairs={{0,1},{1,0},{2,3},{3,2},{4,5},{5,4},{6,7},{7,6},{8,9},{9,8},{10,11... | collective-permute-start | bytes 884744 | tf_op jit(solution)/shard_map/ppermute | solution.py:322
  81.8 1.7 %collective-permute-start.16 = (f32[576,128]{1,0:T(8,128)S(1)}, f32[576,128]{1,0:T(8,128)S(1)}, u32[]{:S(2)}, u32[]{:S(2)}) collective-permute-start(f32[576,128]{1,0:T(8,128)S(1)} %get-tuple-element.44), channel_id=1, source_target_pairs={{0,1},{1,0},{2,3},{3,2},{4,5},{5,4},{6,7},{7,6},{8,9},{9,8},{10,11... | collective-permute-start | bytes 884744 | tf_op jit(solution)/shard_map/ppermute | solution.py:322
